TPU v7x, 32 devices: a whole 2x2x4 slice. The times are simulated.
32 devices in a mesh: ctx: 2 (over core), section: 4 (over y, x), dp: 4 (over z).
Axes of the slice: x: 2, y: 2, z: 4, core: 2. Of those that a mesh axis runs over, the one named last changes fastest.
Arguments:
- conv_input: bfloat16 [4, 4, 256, 5120], P('section', 'dp', 'ctx'), may hold values from -6 to 6
- gate_input: bfloat16 [4, 4, 256, 1024], P('section', 'dp', 'ctx'), may hold values from -6 to 6
- step_input: bfloat16 [4, 4, 256, 16], P('section', 'dp', 'ctx'), may hold values from -7 to 3
- cotangent: bfloat16 [4, 4, 256, 1024], P('section', 'dp', 'ctx'), may hold values from -6 to 6
- conv_weight: float32 [4, 4, 5120], P('section'), may hold values from -3 to 3
- conv_bias: float32 [4, 5120], P('section'), may hold values from -0.5 to 0.5
- step_bias: float32 [4, 16], P('section'), may hold values from -0.5 to 0.5
- decay_log: float32 [4, 16], P('section'), may hold values from -6 to 0.3
- skip_gain: float32 [4, 16], P('section'), may hold values from 0.5 to 1.5
- norm_gain: float32 [4, 1024], P('section'), may hold values from 0.5 to 1.5
Outputs:
- next_input: bfloat16 [4, 4, 256, 1024], P('section', 'dp', 'ctx')
- grad_conv_input: bfloat16 [4, 4, 256, 5120], P('section', 'dp', 'ctx')
- grad_gate_input: bfloat16 [4, 4, 256, 1024], P('section', 'dp', 'ctx')
- grad_step_input: bfloat16 [4, 4, 256, 16], P('section', 'dp', 'ctx')
- kernel_filter_derivative: float32 [4, 4, 5120], P('section')
- grad_conv_bias: float32 [4, 5120], P('section')
- grad_step_bias: float32 [4, 16], P('section')
- grad_decay_log: float32 [4, 16], P('section')
- grad_skip_gain: float32 [4, 16], P('section')
- grad_norm_gain: float32 [4, 1024], P('section')
All inputs are finite; a program needn't handle non-finite values.
Results may differ from a plain program's by a relative error of at most 0.0026.
Values may be sent and summed in bfloat16 or wider, within the bound.
A program may use at most 128 MiB of HBM per device.

v0:
```python
import functools
import jax
import jax.numpy as jnp
from jax import lax
from jax.experimental import pallas as pl
from jax.experimental.pallas import tpu as pltpu
from jax.sharding import PartitionSpec as P

HEADS = 16
HEAD_DIM = 64
STATE = 256
GROUPS = 8
CONV = 4


HIGH_BOUND = lax.Precision.HIGHEST


def shifted(block, axis, distance):
    devices = range(lax.axis_size(axis))
    route = [(i - distance, i) for i in devices if i - distance in devices]
    return lax.ppermute(block, axis, route)


def prefix(part, axis, combine, identity):
    count = lax.axis_size(axis)
    place = lax.axis_index(axis)
    ahead = count - 1 - place
    gathered = jax.tree.map(lambda a: lax.all_gather(a, axis), part)
    state = jax.tree.map(lambda a, e: jnp.zeros_like(a) + jnp.asarray(e, a.dtype), part, identity)

    def one(turn, state):
        source = count - 1 - turn
        return combine(
            state, jax.tree.map(lambda a: lax.dynamic_index_in_dim(a, source, 0, False), gathered)
        )

    return lax.fori_loop(0, ahead, one, state)


def conv_mix(extended, taps, initial_offset):
    rows = extended.shape[0] - (CONV - 1)
    total = initial_offset[None, :]
    for tap in range(CONV):
        total = total + taps[tap][None, :] * extended[tap : tap + rows]
    return jax.nn.silu(total)


def split_mix(mixed, steps, step_shift, damping_exponents):
    rows = mixed.shape[0]
    inner = HEADS * HEAD_DIM
    payload_lines = mixed[:, :inner].reshape(rows, GROUPS, HEADS // GROUPS, HEAD_DIM)
    in_maps = mixed[:, inner : inner + GROUPS * STATE].reshape(rows, GROUPS, STATE)
    out_maps = mixed[:, inner + GROUPS * STATE :].reshape(rows, GROUPS, STATE)
    delta = jax.nn.softplus(steps + step_shift[None, :])
    cumulative = jnp.cumsum(delta * (-jnp.exp(damping_exponents))[None, :], axis=0)
    return (payload_lines, in_maps, out_maps, delta, cumulative)


def fragment_condition(extended, steps, taps, initial_offset, step_shift, damping_exponents):
    payload_lines, in_maps, out_maps, delta, cumulative = split_mix(
        conv_mix(extended, taps, initial_offset), steps, step_shift, damping_exponents
    )
    rows = payload_lines.shape[0]
    total = cumulative[-1]
    weight = (jnp.exp(total[None, :] - cumulative) * delta).reshape(rows, GROUPS, HEADS // GROUPS)
    state = jnp.einsum(
        "tgrp,tgn->grpn", payload_lines * weight[..., None], in_maps, precision=HIGH_BOUND
    )
    return (state.reshape(HEADS, HEAD_DIM, STATE), total)


def shard_layer(
    extended,
    gates,
    steps,
    taps,
    initial_offset,
    step_shift,
    damping_exponents,
    skip_values,
    gain_values,
    carried,
):
    payload_lines, in_maps, out_maps, delta, cumulative = split_mix(
        conv_mix(extended, taps, initial_offset), steps, step_shift, damping_exponents
    )
    rows = payload_lines.shape[0]
    reps = HEADS // GROUPS
    lower = (jnp.arange(rows)[:, None] >= jnp.arange(rows)[None, :])[None]
    seg = cumulative.T[:, :, None] - cumulative.T[:, None, :]
    weight = jnp.exp(jnp.where(lower, seg, -jnp.inf)).reshape(GROUPS, reps, rows, rows)
    intersection_maps = jnp.einsum("tgn,sgn->gts", out_maps, in_maps, precision=HIGH_BOUND)
    score_matrix = weight * intersection_maps[:, None]
    scaled_values = payload_lines * delta.reshape(rows, GROUPS, reps)[..., None]
    final_output = jnp.einsum("jzlh,hjzc->ljzc", score_matrix, scaled_values, precision=HIGH_BOUND)
    incoming = jnp.einsum(
        "tgn,grpn->tgrp",
        out_maps,
        carried.reshape(GROUPS, reps, HEAD_DIM, STATE),
        precision=HIGH_BOUND,
    )
    final_output = (
        final_output + incoming * jnp.exp(cumulative).reshape(rows, GROUPS, reps)[..., None]
    )
    final_output = (
        final_output + skip_values.reshape(GROUPS, reps)[None, :, :, None] * payload_lines
    )
    gated = final_output.reshape(rows, GROUPS, -1) * jax.nn.silu(gates).reshape(rows, GROUPS, -1)
    normed = gated * lax.rsqrt(jnp.mean(gated * gated, axis=-1, keepdims=True) + 1e-05)
    return normed.reshape(rows, -1) * gain_values[None, :]


def combine(earlier, later):
    return (earlier[0] * later[0], later[0][:, None] * earlier[1] + later[1])


def shards(
    conv_input,
    gate_input,
    step_input,
    cotangent,
    conv_weight,
    conv_bias,
    step_bias,
    decay_log,
    skip_gain,
    norm_gain,
):
    local_rows = conv_input[0, 0]
    count = local_rows.shape[0]
    taps, initial_offset = (conv_weight[0], conv_bias[0])
    step_shift, damping_exponents = (step_bias[0], decay_log[0])
    skip_values, gain_values = (skip_gain[0], norm_gain[0])
    previous = shifted(local_rows[count - (CONV - 1) :], "ctx", 1)
    extended = jnp.concatenate([previous, local_rows], 0).astype(jnp.float32)
    gates = gate_input[0, 0].astype(jnp.float32)
    steps = step_input[0, 0].astype(jnp.float32)
    (state, total), state_pull = jax.vjp(
        fragment_condition, extended, steps, taps, initial_offset, step_shift, damping_exponents
    )
    decay = jnp.exp(total)
    flat_state = state.reshape(HEADS, HEAD_DIM * STATE)
    unity = (jnp.ones((HEADS,), jnp.float32), jnp.zeros((HEADS, HEAD_DIM * STATE), jnp.float32))

    def advance(index, current):
        return shifted(decay[:, None] * current + flat_state, "ctx", 1)

    incoming = lax.fori_loop(
        0, lax.axis_size("ctx") - 1, advance, jnp.zeros((HEADS, HEAD_DIM * STATE), jnp.float32)
    )
    carried = incoming.reshape(HEADS, HEAD_DIM, STATE)
    final_output, layer_pull = jax.vjp(
        shard_layer,
        extended,
        gates,
        steps,
        taps,
        initial_offset,
        step_shift,
        damping_exponents,
        skip_values,
        gain_values,
        carried,
    )
    forward = shifted(final_output.astype(jnp.bfloat16)[None, None], "section", 1)
    grads = layer_pull(cotangent[0, 0].astype(jnp.float32))
    carry_grad = grads[9].reshape(HEADS, HEAD_DIM * STATE)
    outgoing = prefix((decay, carry_grad), "ctx", combine, unity)[1]
    outgoing_grad = outgoing.reshape(HEADS, HEAD_DIM, STATE)
    total_grad = jnp.sum(outgoing_grad * carried, axis=(1, 2)) * decay
    extra = state_pull((outgoing_grad, total_grad))
    ext_grad = grads[0] + extra[0]
    step_grad = grads[2] + extra[1]
    param_terms = (
        grads[3] + extra[2],
        grads[4] + extra[3],
        grads[5] + extra[4],
        grads[6] + extra[5],
        grads[7],
        grads[8],
    )
    returned = shifted(ext_grad[: CONV - 1], "ctx", -1)
    own_grad = ext_grad[CONV - 1 :]
    row_grad = jnp.concatenate(
        [own_grad[: count - (CONV - 1)], own_grad[count - (CONV - 1) :] + returned], 0
    )
    backward = shifted(
        (
            row_grad.astype(jnp.bfloat16)[None, None],
            grads[1].astype(jnp.bfloat16)[None, None],
            step_grad.astype(jnp.bfloat16)[None, None],
        ),
        "section",
        -1,
    )
    summed = lax.psum(
        (
            param_terms[0],
            param_terms[1],
            param_terms[2],
            param_terms[3],
            param_terms[4],
            param_terms[5],
        ),
        ("ctx", "dp"),
    )
    return (
        forward,
        backward[0],
        backward[1],
        backward[2],
        summed[0][None],
        summed[1][None],
        summed[2][None],
        summed[3][None],
        summed[4][None],
        summed[5][None],
    )


MESH = pl.DeviceIdType.MESH
F32 = jnp.float32
BF16 = jnp.bfloat16
INNER = HEADS * HEAD_DIM
REPS = HEADS // GROUPS
WIDE = REPS * HEAD_DIM
MIX = WIDE + 2 * STATE
HALF = GROUPS // 2
NN = ((1,), (0,))
NT = ((1,), (1,))
TN = ((0,), (0,))


def split(a):
    high = a.astype(BF16)
    return high, (a - high.astype(F32)).astype(BF16)


def dot(a, b, dims):
    return lax.dot_general(a, b, (dims, ((), ())), preferred_element_type=F32)


def dot3(a, b, dims):
    return dot(a[0], b[0], dims) + (dot(a[0], b[1], dims) + dot(a[1], b[0], dims))


def group_columns(g):
    return (
        pl.multiple_of(g * WIDE, 128),
        pl.multiple_of(INNER + g * STATE, 128),
        pl.multiple_of(INNER + (GROUPS + g) * STATE, 128),
    )


def pair_kernel(
    conv_in, gate_in, step_in, cot_in, w_ref, b_ref, sb_ref, dl_ref, sk_ref, ng_ref,
    nxt, gconv, ggate, gstep, packed,
    uin, steps, steprow, upad, zpad, mix, dsl, dtc, sigc, ratec, cumc, cumr, ddt, drate, small,
    stage_c, stage_o, stage_s, step_parts, partial, final, zeros, relay, step_out,
    own_sem, xs_sem, xr_sem, st_sem, conv_sem, gate_sem, next_sem, dstep_sem,
    ps_sem, pr_sem, fin_sem, zero_sem, via_sem, relay_sem,
):
    core = lax.axis_index("ctx")
    sec = lax.axis_index("section")
    dp = lax.axis_index("dp")
    nsec = lax.axis_size("section")
    ndp = lax.axis_size("dp")
    tok = conv_in.shape[2]
    seq = 2 * tok
    other = 1 - core

    def place(c, s, d):
        return {"ctx": c, "section": s, "dp": d}

    def remote(src, dst, send, recv, c, s, d):
        return pltpu.make_async_remote_copy(
            src_ref=src, dst_ref=dst, send_sem=send, recv_sem=recv,
            device_id=place(c, s, d), device_id_type=MESH,
        )

    after = lax.rem(sec + 1, nsec)
    before = lax.rem(sec + nsec - 1, nsec)
    barrier = pltpu.get_barrier_semaphore()

    def greet(c, s, d):
        pl.semaphore_signal(barrier, inc=1, device_id=place(c, s, d), device_id_type=MESH)

    greet(other, sec, dp)
    for c in range(2):
        greet(c, after, dp)
        greet(c, before, dp)
        greet(c, lax.rem(sec + 2, nsec), dp)
    for k in range(1, ndp):
        greet(core, sec, lax.rem(dp + k, ndp))

    def pieces(g):
        xc, bc, cc = group_columns(g)
        return (
            (conv_in.at[0, 0, :, pl.ds(xc, WIDE)], 0, WIDE),
            (conv_in.at[0, 0, :, pl.ds(bc, STATE)], WIDE, STATE),
            (conv_in.at[0, 0, :, pl.ds(cc, STATE)], WIDE + STATE, STATE),
            (gate_in.at[0, 0, :, pl.ds(xc, WIDE)], MIX, WIDE),
            (cot_in.at[0, 0, :, pl.ds(xc, WIDE)], MIX + WIDE, WIDE),
        )

    mine = pl.ds(pl.multiple_of(core * tok, tok), tok)
    theirs = pl.ds(pl.multiple_of(other * tok, tok), tok)
    own_step = pltpu.make_async_copy(step_in.at[0, 0], steps.at[core], st_sem.at[0])
    own_step.start()

    def fetch(j, _):
        for src, off, width in pieces(core * HALF + j):
            pltpu.make_async_copy(
                src, uin.at[j, mine, pl.ds(off, width)], own_sem.at[j]
            ).start()
        return 0

    lax.fori_loop(0, HALF, fetch, 0)
    zeros[...] = jnp.zeros_like(zeros)
    partial[dp] = jnp.zeros(partial.shape[1:], F32)
    upad[0:8, :] = jnp.zeros((8, MIX), F32)
    zpad[seq : seq + 8, :] = jnp.zeros((8, MIX), F32)
    for ref in (steprow, dtc, sigc, ratec, ddt, drate, small):
        ref[...] = jnp.zeros_like(ref)
    pl.semaphore_wait(barrier, 1 + 6 + (ndp - 1))
    step_copy = remote(
        step_in.at[0, 0], steps.at[core], st_sem.at[1], st_sem.at[2], other, sec, dp
    )
    step_copy.start()

    def exchange(j, _):
        for src, off, width in pieces(other * HALF + j):
            remote(
                src, uin.at[j, mine, pl.ds(off, width)], xs_sem.at[j], xr_sem.at[j], other, sec, dp
            ).start()
        return 0

    lax.fori_loop(0, HALF, exchange, 0)

    @pl.when(sec == 0)
    def _():
        pltpu.make_async_copy(zeros, nxt.at[0, 0], zero_sem.at[0]).start()

    @pl.when(sec == nsec - 1)
    def _():
        for part in range(5):
            pltpu.make_async_copy(
                zeros, gconv.at[0, 0, :, pl.ds(part * INNER, INNER)], zero_sem.at[1]
            ).start()
        pltpu.make_async_copy(zeros, ggate.at[0, 0], zero_sem.at[2]).start()

    own_step.wait()
    step_copy.wait()
    for c in range(2):
        steprow[0:HEADS, c * tok : (c + 1) * tok] = steps[c].astype(F32)
    raw = steprow[...].T[:, 0:HEADS] + sb_ref[...]
    delta = jnp.maximum(raw, 0.0) + jnp.log1p(jnp.exp(-jnp.abs(raw)))
    dtc[:, 0:HEADS] = delta
    sigc[:, 0:HEADS] = jax.nn.sigmoid(raw)
    ratec[:, 0:HEADS] = delta * (-jnp.exp(dl_ref[...]))
    rows2 = lax.broadcasted_iota(jnp.int32, (seq, seq), 0)
    cols2 = lax.broadcasted_iota(jnp.int32, (seq, seq), 1)
    ones_low = jnp.where(rows2 >= cols2, 1.0, 0.0).astype(BF16)
    rate = ratec[...]
    r_hi, r_rest = rate.astype(BF16), rate - rate.astype(BF16).astype(F32)
    r_mid, r_lo = split(r_rest)
    cumulative = dot(ones_low, r_hi, NN) + (dot(ones_low, r_mid, NN) + dot(ones_low, r_lo, NN))
    cumc[...] = cumulative
    cumr[...] = cumulative.T

    def group(j, _):
        g = core * HALF + j
        cols = group_columns(g)
        pltpu.make_async_copy(uin.at[j, mine], uin.at[j, mine], own_sem.at[j]).wait()
        remote(uin.at[j, mine], uin.at[j, theirs], xs_sem.at[j], xr_sem.at[j], other, sec, dp).wait()
        blocks = [(0, cols[0])]
        for base, col in ((WIDE, cols[1]), (WIDE + STATE, cols[2])):
            for part in range(STATE // 128):
                blocks.append((base + part * 128, pl.multiple_of(col + part * 128, 128)))

        for off, col in blocks:
            here = slice(off, off + 128)
            upad[8 : 8 + seq, here] = uin[j, :, here].astype(F32)
            z = b_ref[:, pl.ds(col, 128)]
            for k in range(CONV):
                z = z + w_ref[0, pl.ds(k, 1), pl.ds(col, 128)] * upad[5 + k : 5 + k + seq, here]
            s = jax.nn.sigmoid(z)
            mix[:, here] = z * s
            dsl[:, here] = s * (1.0 + z * (1.0 - s))

        lane = lax.broadcasted_iota(jnp.int32, (seq, 128), 1)
        lane1 = lax.broadcasted_iota(jnp.int32, (1, 128), 1)
        lane16 = lax.broadcasted_iota(jnp.int32, (1, HEADS), 1)
        row = lax.broadcasted_iota(jnp.int32, (seq, seq), 0)
        column = lax.broadcasted_iota(jnp.int32, (seq, seq), 1)
        first = lane < HEAD_DIM

        def pick(ref, h):
            return jnp.sum(jnp.where(lane == h, ref[...], 0.0), axis=1, keepdims=True)

        def pick1(ref, h):
            return jnp.sum(jnp.where(lane16 == h, ref[...], 0.0), axis=1, keepdims=True)

        x = mix[:, 0:WIDE]
        bmap = split(mix[:, WIDE : WIDE + STATE])
        cmap = split(mix[:, WIDE + STATE : MIX])
        h0 = g * REPS
        dt2 = jnp.where(first, pick(dtc, h0), pick(dtc, h0 + 1))
        skip2 = jnp.where(first[0:1], pick1(sk_ref, h0), pick1(sk_ref, h0 + 1))
        xs = x * dt2
        xs_p = split(xs)
        scores = dot3(cmap, bmap, NT)
        decay, mixed, ys = [], [], []
        for r in range(REPS):
            seg = pick(cumc, h0 + r) - cumr[pl.ds(h0 + r, 1), :]
            w = jnp.exp(jnp.where(row >= column, seg, -jnp.inf))
            a = scores * w
            a_p = split(a)
            decay.append(w)
            mixed.append((a, a_p))
            ys.append(dot3(a_p, xs_p, NN))
        y = jnp.where(first, ys[0], ys[1]) + skip2 * x
        gate = uin[j, :, MIX : MIX + WIDE].astype(F32)
        cot = uin[j, :, MIX + WIDE : MIX + 2 * WIDE].astype(F32)
        gain = ng_ref[:, pl.ds(cols[0], WIDE)]
        s = jax.nn.sigmoid(gate)
        act = gate * s
        gated = y * act
        scale = lax.rsqrt(jnp.mean(gated * gated, axis=1, keepdims=True) + 1e-05)
        normed = gated * scale
        stage_o[j, :, 0:WIDE] = (normed * gain).astype(BF16)
        dn = cot * gain
        dgated = scale * (dn - normed * jnp.mean(dn * normed, axis=1, keepdims=True))
        dy = dgated * act
        stage_o[j, :, WIDE : 2 * WIDE] = (dgated * y * (s * (1.0 + gate * (1.0 - s)))).astype(BF16)

        odd = lax.rem(j, 2) == 1

        def send_half(base, t, dst, done, landed, s):
            remote(
                stage_o.at[j, pl.ds(t * tok, tok), pl.ds(base, WIDE)], dst, done, landed, t, s, dp
            ).start()

        @pl.when(jnp.logical_and(sec < nsec - 1, jnp.logical_not(jnp.logical_and(sec == 1, odd))))
        def _():
            for t in range(2):
                send_half(
                    0, t, nxt.at[0, 0, :, pl.ds(cols[0], WIDE)],
                    next_sem.at[0], next_sem.at[1], sec + 1,
                )

        @pl.when(jnp.logical_and(sec == 1, odd))
        def _():
            slot = core * (HALF // 2) + j // 2
            for t in range(2):
                send_half(0, t, relay.at[slot], next_sem.at[0], relay_sem.at[slot], 3)

        @pl.when(jnp.logical_or(sec == 1, sec == 3))
        def _():
            for t in range(2):
                send_half(
                    WIDE, t, ggate.at[0, 0, :, pl.ds(cols[0], WIDE)],
                    gate_sem.at[0], gate_sem.at[1], sec - 1,
                )

        @pl.when(sec == 2)
        def _():
            slot = core * HALF + j
            for t in range(2):
                send_half(WIDE, t, relay.at[slot], gate_sem.at[0], relay_sem.at[slot], 0)

        partial[dp, j, 5:6, 0:WIDE] = jnp.sum(cot * normed, axis=0, keepdims=True)
        dyx = jnp.sum(dy * x, axis=0, keepdims=True)
        dscore = jnp.zeros((seq, seq), F32)
        dy_p = split(dy)
        das = []
        for r in range(REPS):
            own = first if r == 0 else jnp.logical_not(first)
            da = dot3(split(jnp.where(own, dy, 0.0)), xs_p, NT)
            das.append(da)
            dscore = dscore + da * decay[r]
        ds_p = split(dscore)

        def conv_back(off, width, start):
            for part in range(width // 128):
                here = slice(off + part * 128, off + part * 128 + 128)
                col = pl.multiple_of(start + part * 128, 128)
                dz = zpad[0:seq, here]
                du = jnp.zeros((seq, 128), F32)
                for k in range(CONV):
                    du = du + w_ref[0, pl.ds(k, 1), pl.ds(col, 128)] * zpad[3 - k : 3 - k + seq, here]
                    partial[dp, j, pl.ds(k, 1), here] = jnp.sum(
                        dz * upad[5 + k : 5 + k + seq, here], axis=0, keepdims=True
                    )
                partial[dp, j, pl.ds(4, 1), here] = jnp.sum(dz, axis=0, keepdims=True)
                stage_c[j, :, here] = du.astype(BF16)

            @pl.when(sec > 0)
            def _():
                for t in range(2):
                    remote(
                        stage_c.at[j, pl.ds(t * tok, tok), pl.ds(off, width)],
                        gconv.at[0, 0, :, pl.ds(start, width)],
                        conv_sem.at[0], conv_sem.at[1], t, sec - 1, dp,
                    ).start()

        zpad[0:seq, WIDE + STATE : MIX] = dot3(ds_p, bmap, NN) * dsl[:, WIDE + STATE : MIX]
        conv_back(WIDE + STATE, STATE, cols[2])
        zpad[0:seq, WIDE : WIDE + STATE] = dot3(ds_p, cmap, TN) * dsl[:, WIDE : WIDE + STATE]
        conv_back(WIDE, STATE, cols[1])
        dxs = jnp.where(first, dot3(mixed[0][1], dy_p, TN), dot3(mixed[1][1], dy_p, TN))
        zpad[0:seq, 0:WIDE] = (skip2 * dy + dxs * dt2) * dsl[:, 0:WIDE]
        conv_back(0, WIDE, cols[0])
        upper = jnp.where(row <= column, 1.0, 0.0).astype(BF16)
        dxx = dxs * x
        for r in range(REPS):
            own = first if r == 0 else jnp.logical_not(first)
            p = split(das[r] * mixed[r][0])
            later = dot(upper, p[0], NN) + dot(upper, p[1], NN)
            dr = jnp.sum(jnp.where(row > column, later, 0.0), axis=1, keepdims=True)
            drate[...] += jnp.where(lane == h0 + r, dr, 0.0)
            total = jnp.sum(jnp.where(own[0:1], dyx, 0.0), axis=1, keepdims=True)
            small[2:3, :] += jnp.where(lane1 == h0 + r, total, 0.0)
            dd = jnp.sum(jnp.where(own, dxx, 0.0), axis=1, keepdims=True)
            ddt[...] += jnp.where(lane == h0 + r, dd, 0.0)

        for k in range(1, ndp):
            to = lax.rem(dp + k, ndp)
            remote(
                partial.at[dp, j], partial.at[dp, j], ps_sem.at[to], pr_sem.at[dp], core, sec, to
            ).start()
        return 0

    lax.fori_loop(0, HALF, group, 0)

    def pass_on(slot, g, out, landed, s):
        part = relay.at[slot]
        remote(part, part, via_sem.at[0], relay_sem.at[slot], core, s, dp).wait_recv()
        remote(
            part, out.at[0, 0, :, pl.ds(g * WIDE, WIDE)], via_sem.at[0], landed, core, s, dp
        ).start()

    @pl.when(sec == 0)
    def _():
        for g in range(GROUPS):
            pass_on(g, g, ggate, gate_sem.at[1], 1)

    @pl.when(sec == 3)
    def _():
        for at in range(GROUPS // 2):
            pass_on(at, 2 * at + 1, nxt, next_sem.at[1], 2)

    damp = jnp.exp(dl_ref[...])
    dr16 = drate[:, 0:HEADS]
    dstep = (ddt[:, 0:HEADS] - dr16 * damp) * sigc[:, 0:HEADS]
    small[0:1, 0:HEADS] = jnp.sum(dstep, axis=0, keepdims=True)
    small[1:2, 0:HEADS] = jnp.sum(dr16 * ratec[:, 0:HEADS], axis=0, keepdims=True)
    drate[:, 0:HEADS] = dstep
    turned = drate[...].T
    for t in range(2):
        stage_s[t] = turned[0:HEADS, t * tok : (t + 1) * tok].astype(BF16)

    @pl.when(sec > 0)
    def _():
        for t in range(2):
            remote(
                stage_s.at[t], step_parts.at[core],
                dstep_sem.at[2], dstep_sem.at[core], t, sec - 1, dp,
            ).start()

    partial[dp, HALF, :, 0:128] = small[...]
    for k in range(1, ndp):
        to = lax.rem(dp + k, ndp)
        remote(
            partial.at[dp, HALF], partial.at[dp, HALF], ps_sem.at[to], pr_sem.at[dp], core, sec, to
        ).start()
    for k in range(1, ndp):
        to = lax.rem(dp + k, ndp)
        remote(partial.at[dp], partial.at[to], ps_sem.at[to], pr_sem.at[to], core, sec, to).wait()
    total = partial[0]
    for k in range(1, ndp):
        total = total + partial[k]
    final[core] = total
    halves = remote(final.at[core], final.at[core], fin_sem.at[0], fin_sem.at[1], other, sec, dp)
    halves.start()
    remote(final.at[core], final.at[other], fin_sem.at[0], fin_sem.at[1], other, sec, dp).wait()
    to_packed = pltpu.make_async_copy(final, packed, own_sem.at[0])
    to_packed.start()

    @pl.when(sec == nsec - 1)
    def _():
        step_out[...] = jnp.zeros_like(step_out)

    @pl.when(sec < nsec - 1)
    def _():
        for c in range(2):
            part = step_parts.at[c]
            remote(part, part, dstep_sem.at[2], dstep_sem.at[c], core, sec + 1, dp).wait_recv()
        step_out[...] = (step_parts[0].astype(F32) + step_parts[1].astype(F32)).astype(BF16)

    to_step = pltpu.make_async_copy(step_out, gstep.at[0, 0], own_sem.at[1])
    to_step.start()

    @pl.when(sec == 0)
    def _():
        pltpu.make_async_copy(zeros, nxt.at[0, 0], zero_sem.at[0]).wait()
        remote(relay, relay, via_sem.at[0], relay_sem.at[0], core, 1, dp).wait_send()

    @pl.when(sec > 0)
    def _():
        low = sec - 1
        remote(stage_c, stage_c, conv_sem.at[0], conv_sem.at[1], core, low, dp).wait_send()
        half_o = stage_o.at[:, :, pl.ds(0, WIDE)]
        remote(half_o, half_o, gate_sem.at[0], gate_sem.at[1], core, low, dp).wait_send()
        remote(stage_s, stage_s, dstep_sem.at[2], dstep_sem.at[0], core, low, dp).wait_send()
        remote(
            nxt.at[0, 0], nxt.at[0, 0], next_sem.at[0], next_sem.at[1], core, low, dp
        ).wait_recv()

    @pl.when(sec == nsec - 1)
    def _():
        whole = gconv.at[0, 0]
        pltpu.make_async_copy(whole, whole, zero_sem.at[1]).wait()
        pltpu.make_async_copy(zeros, ggate.at[0, 0], zero_sem.at[2]).wait()
        used = relay.at[pl.ds(0, GROUPS // 2)]
        remote(used, used, via_sem.at[0], relay_sem.at[0], core, 2, dp).wait_send()

    @pl.when(sec < nsec - 1)
    def _():
        high = sec + 1
        half_o = stage_o.at[:, :, pl.ds(0, WIDE)]
        remote(half_o, half_o, next_sem.at[0], next_sem.at[1], core, high, dp).wait_send()
        whole = ggate.at[0, 0]
        remote(whole, whole, gate_sem.at[0], gate_sem.at[1], core, high, dp).wait_recv()
        whole = gconv.at[0, 0]
        remote(whole, whole, conv_sem.at[0], conv_sem.at[1], core, high, dp).wait_recv()

    to_packed.wait()
    to_step.wait()


def finish_kernel(
    nxt_in, gconv_in, ggate_in, gstep_in, packed_in,
    nxt, gconv, ggate, gstep, gtap, gcb, gsb, gdl, gsk, gng,
    held, held_step, packed, in_sem, out_sem,
):
    routes = [
        (gstep_in.at[0, 0], held_step, gstep.at[0, 0]),
        (nxt_in.at[0, 0], held.at[0], nxt.at[0, 0]),
        (ggate_in.at[0, 0], held.at[1], ggate.at[0, 0]),
    ]
    for part in range(5):
        cut = pl.ds(part * INNER, INNER)
        routes.append((gconv_in.at[0, 0, :, cut], held.at[2 + part], gconv.at[0, 0, :, cut]))
    arrive = [pltpu.make_async_copy(a, b, in_sem.at[i]) for i, (a, b, _) in enumerate(routes)]
    leave = [pltpu.make_async_copy(b, c, out_sem.at[i]) for i, (_, b, c) in enumerate(routes)]
    first = pltpu.make_async_copy(packed_in, packed, in_sem.at[8])
    first.start()
    for copy in arrive:
        copy.start()
    for into, out in zip(arrive, leave):
        into.wait()
        out.start()
    first.wait()
    for g in range(GROUPS):
        c, j = g // HALF, g % HALF
        gng[0:1, g * WIDE : (g + 1) * WIDE] = packed[c, j, 5:6, 0:WIDE]
        for off, width, col in (
            (0, WIDE, g * WIDE),
            (WIDE, STATE, INNER + g * STATE),
            (WIDE + STATE, STATE, INNER + (GROUPS + g) * STATE),
        ):
            gtap[0, :, col : col + width] = packed[c, j, 0:CONV, off : off + width]
            gcb[0:1, col : col + width] = packed[c, j, CONV : CONV + 1, off : off + width]
    for at, ref in enumerate((gsb, gdl, gsk)):
        ref[...] = packed[0, HALF, at : at + 1, 0:HEADS] + packed[1, HALF, at : at + 1, 0:HEADS]
    for out in leave:
        out.wait()


def paired(
    conv_input, gate_input, step_input, cotangent, conv_weight,
    conv_bias, step_bias, decay_log, skip_gain, norm_gain,
):
    tok = conv_input.shape[2]
    seq = 2 * tok
    ndp = lax.axis_size("dp")
    hbm = pl.BlockSpec(memory_space=pl.ANY)
    vmem = pl.BlockSpec(memory_space=pltpu.VMEM)
    like = lambda a, kind: jax.ShapeDtypeStruct(a.shape, kind)
    scratch = [
        pltpu.VMEM((HALF, seq, MIX + 2 * WIDE), BF16),
        pltpu.VMEM((2, HEADS, tok), BF16),
        pltpu.VMEM((128, seq), F32),
        pltpu.VMEM((seq + 8, MIX), F32),
        pltpu.VMEM((seq + 8, MIX), F32),
        pltpu.VMEM((seq, MIX), F32),
        pltpu.VMEM((seq, MIX), F32),
        pltpu.VMEM((seq, 128), F32),
        pltpu.VMEM((seq, 128), F32),
        pltpu.VMEM((seq, 128), F32),
        pltpu.VMEM((seq, 128), F32),
        pltpu.VMEM((128, seq), F32),
        pltpu.VMEM((seq, 128), F32),
        pltpu.VMEM((seq, 128), F32),
        pltpu.VMEM((8, 128), F32),
        pltpu.VMEM((HALF, seq, MIX), BF16),
        pltpu.VMEM((HALF, seq, 2 * WIDE), BF16),
        pltpu.VMEM((2, HEADS, tok), BF16),
        pltpu.VMEM((2, HEADS, tok), BF16),
        pltpu.VMEM((ndp, HALF + 1, 8, MIX), F32),
        pltpu.VMEM((2, HALF + 1, 8, MIX), F32),
        pltpu.VMEM((tok, INNER), BF16),
        pltpu.VMEM((GROUPS, tok, WIDE), BF16),
        pltpu.VMEM((HEADS, tok), BF16),
        pltpu.SemaphoreType.DMA((HALF,)),
        pltpu.SemaphoreType.DMA((HALF,)),
        pltpu.SemaphoreType.DMA((HALF,)),
        pltpu.SemaphoreType.DMA((3,)),
        pltpu.SemaphoreType.DMA((2,)),
        pltpu.SemaphoreType.DMA((2,)),
        pltpu.SemaphoreType.DMA((2,)),
        pltpu.SemaphoreType.DMA((3,)),
        pltpu.SemaphoreType.DMA((ndp,)),
        pltpu.SemaphoreType.DMA((ndp,)),
        pltpu.SemaphoreType.DMA((2,)),
        pltpu.SemaphoreType.DMA((3,)),
        pltpu.SemaphoreType.DMA((1,)),
        pltpu.SemaphoreType.DMA((GROUPS,)),
    ]
    turned = jnp.swapaxes(step_input, 2, 3)
    sent = pl.pallas_call(
        pair_kernel,
        name="mixer_tick",
        in_specs=[hbm] * 4 + [vmem] * 6,
        out_specs=[hbm] * 5,
        out_shape=[
            like(gate_input, BF16),
            like(conv_input, BF16),
            like(gate_input, BF16),
            like(turned, BF16),
            jax.ShapeDtypeStruct((2, HALF + 1, 8, MIX), F32),
        ],
        scratch_shapes=scratch,
        compiler_params=pltpu.CompilerParams(collective_id=0, has_side_effects=True),
    )(
        conv_input, gate_input, turned, cotangent, conv_weight,
        conv_bias, step_bias, decay_log, skip_gain, norm_gain,
    )
    done = pl.pallas_call(
        finish_kernel,
        name="mixer_finish",
        in_specs=[hbm] * 5,
        out_specs=[hbm] * 4 + [vmem] * 6,
        out_shape=[
            like(gate_input, BF16),
            like(conv_input, BF16),
            like(gate_input, BF16),
            like(turned, BF16),
            like(conv_weight, F32),
            like(conv_bias, F32),
            like(step_bias, F32),
            like(decay_log, F32),
            like(skip_gain, F32),
            like(norm_gain, F32),
        ],
        scratch_shapes=[
            pltpu.VMEM((7, tok, INNER), BF16),
            pltpu.VMEM((HEADS, tok), BF16),
            pltpu.VMEM((2, HALF + 1, 8, MIX), F32),
            pltpu.SemaphoreType.DMA((9,)),
            pltpu.SemaphoreType.DMA((8,)),
        ],
    )(*sent)
    return tuple(done[:3]) + (jnp.swapaxes(done[3], 2, 3),) + tuple(done[4:])


def solution(mesh):
    in_specs = (
        P("section", "dp", "ctx", None),
        P("section", "dp", "ctx", None),
        P("section", "dp", "ctx", None),
        P("section", "dp", "ctx", None),
        P("section", None, None),
        P("section", None),
        P("section", None),
        P("section", None),
        P("section", None),
        P("section", None),
    )
    out_specs = (
        P("section", "dp", "ctx", None),
        P("section", "dp", "ctx", None),
        P("section", "dp", "ctx", None),
        P("section", "dp", "ctx", None),
        P("section", None, None),
        P("section", None),
        P("section", None),
        P("section", None),
        P("section", None),
        P("section", None),
    )
    body = paired if (mesh.shape["ctx"], mesh.shape["section"]) == (2, 4) else shards
    return jax.shard_map(body, mesh=mesh, in_specs=in_specs, out_specs=out_specs, check_vma=False)
```

profile of v0, /device:TPU:0, one launch (start us, length us, event | category | flops | bytes accessed | tf_op | source)
XLA Modules:
  0.0 53.0 jit_solution(9391551526008003464)
XLA Ops:
  0.6 49.3 %mixer_tick.1 = (bf16[1,1,128,1024]{3,2,1,0:T(8,128)(2,1)}, bf16[1,1,128,5120]{3,2,1,0:T(8,128)(2,1)}, bf16[1,1,128,1024]{3,2,1,0:T(8,128)(2,1)}, bf16[1,1,16,128]{3,2,1,0:T(8,128)(2,1)}, f32[2,5,8,640]{3,2,1,0:T(8,128)}) custom-call(bf16[1,1,128,5120]{3,2,1,0:T(8,128)(2,1)} %conv_in.1, bf16[1,1,128,1024]{3,2,1,0:T(8,128)(2,1)} %gate_in.1, ...), custom_call_target="tpu_custom_call" | custom-call | tf_op jit(solution)/shard_map/mixer_tick/pallas_call | solution.py:733
  49.9 3.1 %mixer_finish.1 = (bf16[1,1,128,1024]{3,2,1,0:T(8,128)(2,1)}, bf16[1,1,128,5120]{3,2,1,0:T(8,128)(2,1)}, bf16[1,1,128,1024]{3,2,1,0:T(8,128)(2,1)}, bf16[1,1,16,...) custom-call(bf16[1,1,128,1024]{3,2,1,0:T(8,128)(2,1)} %get-tuple-ele, ...), custom_call_target="tpu_custom_call" | custom-call | tf_op jit(solution)/shard_map/mixer_finish/pallas_call | solution.py:751
where the time goes:
time: 53.2 us; the launch traced here: 53 us
  Pallas kernels  52.4 us (98%)
  between operations  0.65 us (1%)
    pallas_call x1, Pallas kernels, paired(): pl.pallas_call(pair_kernel, name='mixer_tick', in_specs=[hbm] * 4 + [vmem...  49.3 us
    pallas_call x1, Pallas kernels, paired(): pl.pallas_call(finish_kernel, name='mixer_finish', in_specs=[hbm] * 5, ou...  3.08 us

commit v1 on v0

--- a/solution.py
+++ b/solution.py
@@ -53,7 +53,9 @@
     in_maps = mixed[:, inner : inner + GROUPS * STATE].reshape(rows, GROUPS, STATE)
     out_maps = mixed[:, inner + GROUPS * STATE :].reshape(rows, GROUPS, STATE)
     delta = jax.nn.softplus(steps + step_shift[None, :])
-    cumulative = jnp.cumsum(delta * (-jnp.exp(damping_exponents))[None, :], axis=0)
+    upto = jnp.tril(jnp.ones((rows, rows), jnp.float32))
+    rates = delta * (-jnp.exp(damping_exponents))[None, :]
+    cumulative = jnp.dot(upto, rates, precision=HIGH_BOUND)
     return (payload_lines, in_maps, out_maps, delta, cumulative)
 
 
@@ -255,11 +257,11 @@
 
 def pair_kernel(
     conv_in, gate_in, step_in, cot_in, w_ref, b_ref, sb_ref, dl_ref, sk_ref, ng_ref,
-    nxt, gconv, ggate, gstep, packed,
+    nxt, gconv, ggate, gstep, gtap, gcb, gsb, gdl, gsk, gng,
     uin, steps, steprow, upad, zpad, mix, dsl, dtc, sigc, ratec, cumc, cumr, ddt, drate, small,
-    stage_c, stage_o, stage_s, step_parts, partial, final, zeros, relay, step_out,
+    stage_c, stage_o, stage_s, step_parts, partial, final, relay,
     own_sem, xs_sem, xr_sem, st_sem, conv_sem, gate_sem, next_sem, dstep_sem,
-    ps_sem, pr_sem, fin_sem, zero_sem, via_sem, relay_sem,
+    ps_sem, pr_sem, fin_sem, via_sem, relay_sem,
 ):
     core = lax.axis_index("ctx")
     sec = lax.axis_index("section")
@@ -317,7 +319,6 @@
         return 0
 
     lax.fori_loop(0, HALF, fetch, 0)
-    zeros[...] = jnp.zeros_like(zeros)
     partial[dp] = jnp.zeros(partial.shape[1:], F32)
     upad[0:8, :] = jnp.zeros((8, MIX), F32)
     zpad[seq : seq + 8, :] = jnp.zeros((8, MIX), F32)
@@ -337,18 +338,6 @@
         return 0
 
     lax.fori_loop(0, HALF, exchange, 0)
-
-    @pl.when(sec == 0)
-    def _():
-        pltpu.make_async_copy(zeros, nxt.at[0, 0], zero_sem.at[0]).start()
-
-    @pl.when(sec == nsec - 1)
-    def _():
-        for part in range(5):
-            pltpu.make_async_copy(
-                zeros, gconv.at[0, 0, :, pl.ds(part * INNER, INNER)], zero_sem.at[1]
-            ).start()
-        pltpu.make_async_copy(zeros, ggate.at[0, 0], zero_sem.at[2]).start()
 
     own_step.wait()
     step_copy.wait()
@@ -551,6 +540,16 @@
         for at in range(GROUPS // 2):
             pass_on(at, 2 * at + 1, nxt, next_sem.at[1], 2)
 
+    @pl.when(sec == 0)
+    def _():
+        nxt[...] = jnp.zeros_like(nxt)
+
+    @pl.when(sec == nsec - 1)
+    def _():
+        gconv[...] = jnp.zeros_like(gconv)
+        ggate[...] = jnp.zeros_like(ggate)
+        gstep[...] = jnp.zeros_like(gstep)
+
     damp = jnp.exp(dl_ref[...])
     dr16 = drate[:, 0:HEADS]
     dstep = (ddt[:, 0:HEADS] - dr16 * damp) * sigc[:, 0:HEADS]
@@ -585,26 +584,28 @@
     halves = remote(final.at[core], final.at[core], fin_sem.at[0], fin_sem.at[1], other, sec, dp)
     halves.start()
     remote(final.at[core], final.at[other], fin_sem.at[0], fin_sem.at[1], other, sec, dp).wait()
-    to_packed = pltpu.make_async_copy(final, packed, own_sem.at[0])
-    to_packed.start()
-
-    @pl.when(sec == nsec - 1)
-    def _():
-        step_out[...] = jnp.zeros_like(step_out)
+    for g in range(GROUPS):
+        c, j = g // HALF, g % HALF
+        gng[0:1, g * WIDE : (g + 1) * WIDE] = final[c, j, 5:6, 0:WIDE]
+        for off, width, col in (
+            (0, WIDE, g * WIDE),
+            (WIDE, STATE, INNER + g * STATE),
+            (WIDE + STATE, STATE, INNER + (GROUPS + g) * STATE),
+        ):
+            gtap[0, :, col : col + width] = final[c, j, 0:CONV, off : off + width]
+            gcb[0:1, col : col + width] = final[c, j, CONV : CONV + 1, off : off + width]
+    for at, ref in enumerate((gsb, gdl, gsk)):
+        ref[...] = final[0, HALF, at : at + 1, 0:HEADS] + final[1, HALF, at : at + 1, 0:HEADS]
 
     @pl.when(sec < nsec - 1)
     def _():
         for c in range(2):
             part = step_parts.at[c]
             remote(part, part, dstep_sem.at[2], dstep_sem.at[c], core, sec + 1, dp).wait_recv()
-        step_out[...] = (step_parts[0].astype(F32) + step_parts[1].astype(F32)).astype(BF16)
-
-    to_step = pltpu.make_async_copy(step_out, gstep.at[0, 0], own_sem.at[1])
-    to_step.start()
+        gstep[0, 0] = (step_parts[0].astype(F32) + step_parts[1].astype(F32)).astype(BF16)
 
     @pl.when(sec == 0)
     def _():
-        pltpu.make_async_copy(zeros, nxt.at[0, 0], zero_sem.at[0]).wait()
         remote(relay, relay, via_sem.at[0], relay_sem.at[0], core, 1, dp).wait_send()
 
     @pl.when(sec > 0)
@@ -620,9 +621,6 @@
 
     @pl.when(sec == nsec - 1)
     def _():
-        whole = gconv.at[0, 0]
-        pltpu.make_async_copy(whole, whole, zero_sem.at[1]).wait()
-        pltpu.make_async_copy(zeros, ggate.at[0, 0], zero_sem.at[2]).wait()
         used = relay.at[pl.ds(0, GROUPS // 2)]
         remote(used, used, via_sem.at[0], relay_sem.at[0], core, 2, dp).wait_send()
 
@@ -636,47 +634,15 @@
         whole = gconv.at[0, 0]
         remote(whole, whole, conv_sem.at[0], conv_sem.at[1], core, high, dp).wait_recv()
 
-    to_packed.wait()
-    to_step.wait()
-
-
-def finish_kernel(
-    nxt_in, gconv_in, ggate_in, gstep_in, packed_in,
-    nxt, gconv, ggate, gstep, gtap, gcb, gsb, gdl, gsk, gng,
-    held, held_step, packed, in_sem, out_sem,
-):
-    routes = [
-        (gstep_in.at[0, 0], held_step, gstep.at[0, 0]),
-        (nxt_in.at[0, 0], held.at[0], nxt.at[0, 0]),
-        (ggate_in.at[0, 0], held.at[1], ggate.at[0, 0]),
-    ]
-    for part in range(5):
-        cut = pl.ds(part * INNER, INNER)
-        routes.append((gconv_in.at[0, 0, :, cut], held.at[2 + part], gconv.at[0, 0, :, cut]))
-    arrive = [pltpu.make_async_copy(a, b, in_sem.at[i]) for i, (a, b, _) in enumerate(routes)]
-    leave = [pltpu.make_async_copy(b, c, out_sem.at[i]) for i, (_, b, c) in enumerate(routes)]
-    first = pltpu.make_async_copy(packed_in, packed, in_sem.at[8])
-    first.start()
-    for copy in arrive:
+
+def finish_kernel(*refs):
+    count = len(refs) // 2
+    sem = refs[-1]
+    copies = [pltpu.make_async_copy(refs[i], refs[count + i], sem.at[i]) for i in range(count)]
+    for copy in copies:
         copy.start()
-    for into, out in zip(arrive, leave):
-        into.wait()
-        out.start()
-    first.wait()
-    for g in range(GROUPS):
-        c, j = g // HALF, g % HALF
-        gng[0:1, g * WIDE : (g + 1) * WIDE] = packed[c, j, 5:6, 0:WIDE]
-        for off, width, col in (
-            (0, WIDE, g * WIDE),
-            (WIDE, STATE, INNER + g * STATE),
-            (WIDE + STATE, STATE, INNER + (GROUPS + g) * STATE),
-        ):
-            gtap[0, :, col : col + width] = packed[c, j, 0:CONV, off : off + width]
-            gcb[0:1, col : col + width] = packed[c, j, CONV : CONV + 1, off : off + width]
-    for at, ref in enumerate((gsb, gdl, gsk)):
-        ref[...] = packed[0, HALF, at : at + 1, 0:HEADS] + packed[1, HALF, at : at + 1, 0:HEADS]
-    for out in leave:
-        out.wait()
+    for copy in copies:
+        copy.wait()
 
 
 def paired(
@@ -688,7 +654,6 @@
     ndp = lax.axis_size("dp")
     hbm = pl.BlockSpec(memory_space=pl.ANY)
     vmem = pl.BlockSpec(memory_space=pltpu.VMEM)
-    like = lambda a, kind: jax.ShapeDtypeStruct(a.shape, kind)
     scratch = [
         pltpu.VMEM((HALF, seq, MIX + 2 * WIDE), BF16),
         pltpu.VMEM((2, HEADS, tok), BF16),
@@ -711,9 +676,7 @@
         pltpu.VMEM((2, HEADS, tok), BF16),
         pltpu.VMEM((ndp, HALF + 1, 8, MIX), F32),
         pltpu.VMEM((2, HALF + 1, 8, MIX), F32),
-        pltpu.VMEM((tok, INNER), BF16),
         pltpu.VMEM((GROUPS, tok, WIDE), BF16),
-        pltpu.VMEM((HEADS, tok), BF16),
         pltpu.SemaphoreType.DMA((HALF,)),
         pltpu.SemaphoreType.DMA((HALF,)),
         pltpu.SemaphoreType.DMA((HALF,)),
@@ -725,53 +688,48 @@
         pltpu.SemaphoreType.DMA((ndp,)),
         pltpu.SemaphoreType.DMA((ndp,)),
         pltpu.SemaphoreType.DMA((2,)),
-        pltpu.SemaphoreType.DMA((3,)),
         pltpu.SemaphoreType.DMA((1,)),
         pltpu.SemaphoreType.DMA((GROUPS,)),
     ]
     turned = jnp.swapaxes(step_input, 2, 3)
+    shapes = [
+        (gate_input.shape, BF16),
+        (conv_input.shape, BF16),
+        (gate_input.shape, BF16),
+        (turned.shape, BF16),
+        (conv_weight.shape, F32),
+        (conv_bias.shape, F32),
+        (step_bias.shape, F32),
+        (decay_log.shape, F32),
+        (skip_gain.shape, F32),
+        (norm_gain.shape, F32),
+    ]
+    inputs = [
+        pltpu.with_memory_space_constraint(a, pltpu.HBM)
+        for a in (
+            conv_input, gate_input, turned, cotangent, conv_weight,
+            conv_bias, step_bias, decay_log, skip_gain, norm_gain,
+        )
+    ]
     sent = pl.pallas_call(
         pair_kernel,
         name="mixer_tick",
         in_specs=[hbm] * 4 + [vmem] * 6,
-        out_specs=[hbm] * 5,
-        out_shape=[
-            like(gate_input, BF16),
-            like(conv_input, BF16),
-            like(gate_input, BF16),
-            like(turned, BF16),
-            jax.ShapeDtypeStruct((2, HALF + 1, 8, MIX), F32),
-        ],
+        out_specs=[vmem] * 10,
+        out_shape=[pltpu.VMEM(shape, kind) for shape, kind in shapes],
         scratch_shapes=scratch,
-        compiler_params=pltpu.CompilerParams(collective_id=0, has_side_effects=True),
-    )(
-        conv_input, gate_input, turned, cotangent, conv_weight,
-        conv_bias, step_bias, decay_log, skip_gain, norm_gain,
-    )
+        compiler_params=pltpu.CompilerParams(
+            collective_id=0, has_side_effects=True, vmem_limit_bytes=24 * 1024 * 1024
+        ),
+    )(*inputs)
     done = pl.pallas_call(
         finish_kernel,
         name="mixer_finish",
-        in_specs=[hbm] * 5,
-        out_specs=[hbm] * 4 + [vmem] * 6,
-        out_shape=[
-            like(gate_input, BF16),
-            like(conv_input, BF16),
-            like(gate_input, BF16),
-            like(turned, BF16),
-            like(conv_weight, F32),
-            like(conv_bias, F32),
-            like(step_bias, F32),
-            like(decay_log, F32),
-            like(skip_gain, F32),
-            like(norm_gain, F32),
-        ],
-        scratch_shapes=[
-            pltpu.VMEM((7, tok, INNER), BF16),
-            pltpu.VMEM((HEADS, tok), BF16),
-            pltpu.VMEM((2, HALF + 1, 8, MIX), F32),
-            pltpu.SemaphoreType.DMA((9,)),
-            pltpu.SemaphoreType.DMA((8,)),
-        ],
+        in_specs=[vmem] * 10,
+        out_specs=[hbm] * 10,
+        out_shape=[jax.ShapeDtypeStruct(shape, kind) for shape, kind in shapes],
+        scratch_shapes=[pltpu.SemaphoreType.DMA((10,))],
+        compiler_params=pltpu.CompilerParams(vmem_limit_bytes=1024 * 1024),
     )(*sent)
     return tuple(done[:3]) + (jnp.swapaxes(done[3], 2, 3),) + tuple(done[4:])
 

time: 53.2 us -> 50.8 us (0.955)
  Pallas kernels: 52.4 us -> 50 us
    pallas_call x1, Pallas kernels: 3.08 us -> 1.35 us  [paired(): pl.pallas_call(finish_kernel, name='mixer_finish', in_specs=[vmem] * 10,...]
    pallas_call x1, Pallas kernels: 49.3 us -> 48.7 us  [paired(): pl.pallas_call(pair_kernel, name='mixer_tick', in_specs=[hbm] * 4 + [vmem...]
where the time goes in v1:
time: 50.8 us; the launch traced here: 50.7 us
  Pallas kernels  50 us (98%)
  between operations  0.65 us (1%)
    pallas_call x1, Pallas kernels, paired(): pl.pallas_call(pair_kernel, name='mixer_tick', in_specs=[hbm] * 4 + [vmem...  48.7 us
    pallas_call x1, Pallas kernels, paired(): pl.pallas_call(finish_kernel, name='mixer_finish', in_specs=[vmem] * 10,...  1.35 us

profile of v1, /device:TPU:0, one launch (start us, length us, event | category | flops | bytes accessed | tf_op | source)
XLA Modules:
  0.0 50.7 jit_solution(7275753248926916955)
XLA Ops:
  0.6 48.7 %mixer_tick.1 = (bf16[1,1,128,1024]{3,2,1,0:T(8,128)(2,1)S(1)}, bf16[1,1,128,5120]{3,2,1,0:T(8,128)(2,1)S(1)}, bf16[1,1,128,1024]{3,2,1,0:T(8,128)(2,1)S(1)}, bf...) custom-call(bf16[1,1,128,5120]{3,2,1,0:T(8,128)(2,1)} %conv_in.1, ...), custom_call_target="tpu_custom_call" | custom-call | tf_op jit(solution)/shard_map/mixer_tick/pallas_call | solution.py:714
  49.3 1.3 %mixer_finish.1 = (bf16[1,1,128,1024]{3,2,1,0:T(8,128)(2,1)}, bf16[1,1,128,5120]{3,2,1,0:T(8,128)(2,1)}, bf16[1,1,128,1024]{3,2,1,0:T(8,128)(2,1)}, bf16[1,1,16,...) custom-call(bf16[1,1,128,1024]{3,2,1,0:T(8,128)(2,1)S(1)} %get-tuple, ...), custom_call_target="tpu_custom_call" | custom-call | tf_op jit(solution)/shard_map/mixer_finish/pallas_call | solution.py:725

commit v2 on v1

--- a/solution.py
+++ b/solution.py
@@ -256,12 +256,13 @@
 
 
 def pair_kernel(
-    conv_in, gate_in, step_in, cot_in, w_ref, b_ref, sb_ref, dl_ref, sk_ref, ng_ref,
+    conv_in, gate_in, step_in, cot_in, w_in, b_in, sb_in, dl_in, sk_in, ng_in,
     nxt, gconv, ggate, gstep, gtap, gcb, gsb, gdl, gsk, gng,
-    uin, steps, steprow, upad, zpad, mix, dsl, dtc, sigc, ratec, cumc, cumr, ddt, drate, small,
+    w_ref, b_ref, sb_ref, dl_ref, sk_ref, ng_ref,
+    uin, steps, token_rows, token_cols, upad, zpad, mix, dsl, ddt, drate, small,
     stage_c, stage_o, stage_s, step_parts, partial, final, relay,
     own_sem, xs_sem, xr_sem, st_sem, conv_sem, gate_sem, next_sem, dstep_sem,
-    ps_sem, pr_sem, fin_sem, via_sem, relay_sem,
+    ps_sem, pr_sem, fin_sem, via_sem, relay_sem, par_sem, plane_sem, world_sem,
 ):
     core = lax.axis_index("ctx")
     sec = lax.axis_index("section")
@@ -288,13 +289,12 @@
     def greet(c, s, d):
         pl.semaphore_signal(barrier, inc=1, device_id=place(c, s, d), device_id_type=MESH)
 
-    greet(other, sec, dp)
     for c in range(2):
-        greet(c, after, dp)
-        greet(c, before, dp)
-        greet(c, lax.rem(sec + 2, nsec), dp)
-    for k in range(1, ndp):
-        greet(core, sec, lax.rem(dp + k, ndp))
+        for s in range(1, 4):
+
+            @pl.when(jnp.logical_or(sec != s, core != c))
+            def _():
+                greet(c, s, dp)
 
     def pieces(g):
         xc, bc, cc = group_columns(g)
@@ -318,13 +318,39 @@
             ).start()
         return 0
 
-    lax.fori_loop(0, HALF, fetch, 0)
+    fetch(0, 0)
+    params = [
+        pltpu.make_async_copy(src, dst, par_sem.at[at])
+        for at, (src, dst) in enumerate((
+            (sb_in, sb_ref), (dl_in, dl_ref), (w_in, w_ref),
+            (b_in, b_ref), (sk_in, sk_ref), (ng_in, ng_ref),
+        ))
+    ]
+    for copy in params:
+        copy.start()
+    lax.fori_loop(1, HALF, fetch, 0)
     partial[dp] = jnp.zeros(partial.shape[1:], F32)
     upad[0:8, :] = jnp.zeros((8, MIX), F32)
     zpad[seq : seq + 8, :] = jnp.zeros((8, MIX), F32)
-    for ref in (steprow, dtc, sigc, ratec, ddt, drate, small):
+    for ref in (token_rows, ddt, drate, small):
         ref[...] = jnp.zeros_like(ref)
-    pl.semaphore_wait(barrier, 1 + 6 + (ndp - 1))
+
+    @pl.when(sec > 0)
+    def _():
+        pl.semaphore_wait(barrier, 7)
+
+    @pl.when(sec == 1)
+    def _():
+        pl.semaphore_signal(
+            plane_sem, inc=1, device_id=place(core, 0, dp), device_id_type=MESH
+        )
+        for k in range(1, ndp):
+            greet(core, 0, lax.rem(dp + k, ndp))
+
+    @pl.when(sec == 0)
+    def _():
+        pl.semaphore_wait(plane_sem, 1)
+
     step_copy = remote(
         step_in.at[0, 0], steps.at[core], st_sem.at[1], st_sem.at[2], other, sec, dp
     )
@@ -338,45 +364,68 @@
         return 0
 
     lax.fori_loop(0, HALF, exchange, 0)
-
-    own_step.wait()
-    step_copy.wait()
-    for c in range(2):
-        steprow[0:HEADS, c * tok : (c + 1) * tok] = steps[c].astype(F32)
-    raw = steprow[...].T[:, 0:HEADS] + sb_ref[...]
-    delta = jnp.maximum(raw, 0.0) + jnp.log1p(jnp.exp(-jnp.abs(raw)))
-    dtc[:, 0:HEADS] = delta
-    sigc[:, 0:HEADS] = jax.nn.sigmoid(raw)
-    ratec[:, 0:HEADS] = delta * (-jnp.exp(dl_ref[...]))
-    rows2 = lax.broadcasted_iota(jnp.int32, (seq, seq), 0)
-    cols2 = lax.broadcasted_iota(jnp.int32, (seq, seq), 1)
-    ones_low = jnp.where(rows2 >= cols2, 1.0, 0.0).astype(BF16)
-    rate = ratec[...]
-    r_hi, r_rest = rate.astype(BF16), rate - rate.astype(BF16).astype(F32)
-    r_mid, r_lo = split(r_rest)
-    cumulative = dot(ones_low, r_hi, NN) + (dot(ones_low, r_mid, NN) + dot(ones_low, r_lo, NN))
-    cumc[...] = cumulative
-    cumr[...] = cumulative.T
+    for copy in params:
+        copy.wait()
+
+    def token_terms():
+        own_step.wait()
+        step_copy.wait()
+        diagonal = lax.broadcasted_iota(jnp.int32, (HEADS, HEADS), 0) == lax.broadcasted_iota(
+            jnp.int32, (HEADS, HEADS), 1
+        )
+
+        def upright(ref):
+            return jnp.sum(jnp.where(diagonal, ref[...], 0.0), axis=1, keepdims=True)
+
+        raw = jnp.concatenate([steps[0].astype(F32), steps[1].astype(F32)], axis=1)
+        raw = raw + upright(sb_ref)
+        delta = jnp.maximum(raw, 0.0) + jnp.log1p(jnp.exp(-jnp.abs(raw)))
+        rate = delta * (-jnp.exp(upright(dl_ref)))
+        rows2 = lax.broadcasted_iota(jnp.int32, (seq, seq), 0)
+        cols2 = lax.broadcasted_iota(jnp.int32, (seq, seq), 1)
+        ones_up = jnp.where(rows2 <= cols2, 1.0, 0.0).astype(BF16)
+        r_hi, r_rest = rate.astype(BF16), rate - rate.astype(BF16).astype(F32)
+        r_mid, r_lo = split(r_rest)
+        cumulative = dot(r_hi, ones_up, NN) + (dot(r_mid, ones_up, NN) + dot(r_lo, ones_up, NN))
+        token_rows[0:HEADS, :] = delta
+        token_rows[HEADS : 2 * HEADS, :] = cumulative
+        token_rows[2 * HEADS : 3 * HEADS, :] = jax.nn.sigmoid(raw)
+        token_rows[3 * HEADS : 4 * HEADS, :] = rate
+        token_cols[...] = token_rows[...].T
 
     def group(j, _):
         g = core * HALF + j
         cols = group_columns(g)
-        pltpu.make_async_copy(uin.at[j, mine], uin.at[j, mine], own_sem.at[j]).wait()
-        remote(uin.at[j, mine], uin.at[j, theirs], xs_sem.at[j], xr_sem.at[j], other, sec, dp).wait()
         blocks = [(0, cols[0])]
         for base, col in ((WIDE, cols[1]), (WIDE + STATE, cols[2])):
             for part in range(STATE // 128):
                 blocks.append((base + part * 128, pl.multiple_of(col + part * 128, 128)))
 
-        for off, col in blocks:
-            here = slice(off, off + 128)
-            upad[8 : 8 + seq, here] = uin[j, :, here].astype(F32)
-            z = b_ref[:, pl.ds(col, 128)]
-            for k in range(CONV):
-                z = z + w_ref[0, pl.ds(k, 1), pl.ds(col, 128)] * upad[5 + k : 5 + k + seq, here]
-            s = jax.nn.sigmoid(z)
-            mix[:, here] = z * s
-            dsl[:, here] = s * (1.0 + z * (1.0 - s))
+        def conv_rows(start, count, fresh):
+            for off, col in blocks:
+                here = slice(off, off + 128)
+                if fresh:
+                    upad[pl.ds(pl.multiple_of(start + 8, 8), count), here] = uin[
+                        j, pl.ds(start, count), here
+                    ].astype(F32)
+                window = upad[pl.ds(start, count + 8), here]
+                z = b_ref[:, pl.ds(col, 128)] + w_ref[0, 3:4, pl.ds(col, 128)] * window[8:]
+                for k in range(CONV - 1):
+                    z = z + w_ref[0, pl.ds(k, 1), pl.ds(col, 128)] * pltpu.roll(window, 3 - k, 0)[8:]
+                s = jax.nn.sigmoid(z)
+                mix[pl.ds(start, count), here] = z * s
+                dsl[pl.ds(start, count), here] = s * (1.0 + z * (1.0 - s))
+
+        pltpu.make_async_copy(uin.at[j, mine], uin.at[j, mine], own_sem.at[j]).wait()
+        conv_rows(pl.multiple_of(core * tok, tok), tok, True)
+
+        @pl.when(j == 0)
+        def _():
+            token_terms()
+
+        remote(uin.at[j, mine], uin.at[j, theirs], xs_sem.at[j], xr_sem.at[j], other, sec, dp).wait()
+        conv_rows(pl.multiple_of(other * tok, tok), tok, True)
+        conv_rows(tok, 8, False)
 
         lane = lax.broadcasted_iota(jnp.int32, (seq, 128), 1)
         lane1 = lax.broadcasted_iota(jnp.int32, (1, 128), 1)
@@ -385,8 +434,8 @@
         column = lax.broadcasted_iota(jnp.int32, (seq, seq), 1)
         first = lane < HEAD_DIM
 
-        def pick(ref, h):
-            return jnp.sum(jnp.where(lane == h, ref[...], 0.0), axis=1, keepdims=True)
+        def pick(at):
+            return jnp.sum(jnp.where(lane == at, token_cols[...], 0.0), axis=1, keepdims=True)
 
         def pick1(ref, h):
             return jnp.sum(jnp.where(lane16 == h, ref[...], 0.0), axis=1, keepdims=True)
@@ -395,14 +444,14 @@
         bmap = split(mix[:, WIDE : WIDE + STATE])
         cmap = split(mix[:, WIDE + STATE : MIX])
         h0 = g * REPS
-        dt2 = jnp.where(first, pick(dtc, h0), pick(dtc, h0 + 1))
+        dt2 = jnp.where(first, pick(h0), pick(h0 + 1))
         skip2 = jnp.where(first[0:1], pick1(sk_ref, h0), pick1(sk_ref, h0 + 1))
         xs = x * dt2
         xs_p = split(xs)
         scores = dot3(cmap, bmap, NT)
         decay, mixed, ys = [], [], []
         for r in range(REPS):
-            seg = pick(cumc, h0 + r) - cumr[pl.ds(h0 + r, 1), :]
+            seg = pick(HEADS + h0 + r) - token_rows[pl.ds(HEADS + h0 + r, 1), :]
             w = jnp.exp(jnp.where(row >= column, seg, -jnp.inf))
             a = scores * w
             a_p = split(a)
@@ -514,6 +563,18 @@
             dd = jnp.sum(jnp.where(own, dxx, 0.0), axis=1, keepdims=True)
             ddt[...] += jnp.where(lane == h0 + r, dd, 0.0)
 
+        @pl.when(jnp.logical_and(j == 0, sec == 0))
+        def _():
+            pl.semaphore_wait(barrier, ndp - 1)
+            for s in range(1, 4):
+                pl.semaphore_signal(
+                    world_sem, inc=1, device_id=place(core, s, dp), device_id_type=MESH
+                )
+
+        @pl.when(jnp.logical_and(j == 0, sec > 0))
+        def _():
+            pl.semaphore_wait(world_sem, 1)
+
         for k in range(1, ndp):
             to = lax.rem(dp + k, ndp)
             remote(
@@ -552,9 +613,11 @@
 
     damp = jnp.exp(dl_ref[...])
     dr16 = drate[:, 0:HEADS]
-    dstep = (ddt[:, 0:HEADS] - dr16 * damp) * sigc[:, 0:HEADS]
+    dstep = (ddt[:, 0:HEADS] - dr16 * damp) * token_cols[:, 2 * HEADS : 3 * HEADS]
     small[0:1, 0:HEADS] = jnp.sum(dstep, axis=0, keepdims=True)
-    small[1:2, 0:HEADS] = jnp.sum(dr16 * ratec[:, 0:HEADS], axis=0, keepdims=True)
+    small[1:2, 0:HEADS] = jnp.sum(
+        dr16 * token_cols[:, 3 * HEADS : 4 * HEADS], axis=0, keepdims=True
+    )
     drate[:, 0:HEADS] = dstep
     turned = drate[...].T
     for t in range(2):
@@ -655,18 +718,20 @@
     hbm = pl.BlockSpec(memory_space=pl.ANY)
     vmem = pl.BlockSpec(memory_space=pltpu.VMEM)
     scratch = [
+        pltpu.VMEM(conv_weight.shape, F32),
+        pltpu.VMEM(conv_bias.shape, F32),
+        pltpu.VMEM(step_bias.shape, F32),
+        pltpu.VMEM(decay_log.shape, F32),
+        pltpu.VMEM(skip_gain.shape, F32),
+        pltpu.VMEM(norm_gain.shape, F32),
         pltpu.VMEM((HALF, seq, MIX + 2 * WIDE), BF16),
         pltpu.VMEM((2, HEADS, tok), BF16),
         pltpu.VMEM((128, seq), F32),
+        pltpu.VMEM((seq, 128), F32),
         pltpu.VMEM((seq + 8, MIX), F32),
         pltpu.VMEM((seq + 8, MIX), F32),
         pltpu.VMEM((seq, MIX), F32),
         pltpu.VMEM((seq, MIX), F32),
-        pltpu.VMEM((seq, 128), F32),
-        pltpu.VMEM((seq, 128), F32),
-        pltpu.VMEM((seq, 128), F32),
-        pltpu.VMEM((seq, 128), F32),
-        pltpu.VMEM((128, seq), F32),
         pltpu.VMEM((seq, 128), F32),
         pltpu.VMEM((seq, 128), F32),
         pltpu.VMEM((8, 128), F32),
@@ -690,6 +755,9 @@
         pltpu.SemaphoreType.DMA((2,)),
         pltpu.SemaphoreType.DMA((1,)),
         pltpu.SemaphoreType.DMA((GROUPS,)),
+        pltpu.SemaphoreType.DMA((6,)),
+        pltpu.SemaphoreType.REGULAR,
+        pltpu.SemaphoreType.REGULAR,
     ]
     turned = jnp.swapaxes(step_input, 2, 3)
     shapes = [
@@ -714,7 +782,7 @@
     sent = pl.pallas_call(
         pair_kernel,
         name="mixer_tick",
-        in_specs=[hbm] * 4 + [vmem] * 6,
+        in_specs=[hbm] * 10,
         out_specs=[vmem] * 10,
         out_shape=[pltpu.VMEM(shape, kind) for shape, kind in shapes],
         scratch_shapes=scratch,

time: 50.8 us -> 47.6 us (0.937)
  Pallas kernels: 50 us -> 46.8 us
    pallas_call x1, Pallas kernels: 48.7 us -> 45.4 us  [paired(): pl.pallas_call(pair_kernel, name='mixer_tick', in_specs=[hbm] * 10, out_s...]
where the time goes in v2:
time: 47.6 us; the launch traced here: 47.4 us
  Pallas kernels  46.8 us (98%)
  between operations  0.65 us (1%)
    pallas_call x1, Pallas kernels, paired(): pl.pallas_call(pair_kernel, name='mixer_tick', in_specs=[hbm] * 10, out_s...  45.4 us
    pallas_call x1, Pallas kernels, paired(): pl.pallas_call(finish_kernel, name='mixer_finish', in_specs=[vmem] * 10,...  1.35 us

profile of v2, /device:TPU:0, one launch (start us, length us, event | category | flops | bytes accessed | tf_op | source)
XLA Modules:
  0.0 47.4 jit_solution(11938618498091653189)
XLA Ops:
  0.6 45.4 %mixer_tick.1 = (bf16[1,1,128,1024]{3,2,1,0:T(8,128)(2,1)S(1)}, bf16[1,1,128,5120]{3,2,1,0:T(8,128)(2,1)S(1)}, bf16[1,1,128,1024]{3,2,1,0:T(8,128)(2,1)S(1)}, bf...) custom-call(bf16[1,1,128,5120]{3,2,1,0:T(8,128)(2,1)} %conv_in.1, ...), custom_call_target="tpu_custom_call" | custom-call | tf_op jit(solution)/shard_map/mixer_tick/pallas_call | solution.py:782
  46.1 1.3 %mixer_finish.1 = (bf16[1,1,128,1024]{3,2,1,0:T(8,128)(2,1)}, bf16[1,1,128,5120]{3,2,1,0:T(8,128)(2,1)}, bf16[1,1,128,1024]{3,2,1,0:T(8,128)(2,1)}, bf16[1,1,16,...) custom-call(bf16[1,1,128,1024]{3,2,1,0:T(8,128)(2,1)S(1)} %get-tuple, ...), custom_call_target="tpu_custom_call" | custom-call | tf_op jit(solution)/shard_map/mixer_finish/pallas_call | solution.py:793

commit v3 on v2

--- a/solution.py
+++ b/solution.py
@@ -260,9 +260,10 @@
     nxt, gconv, ggate, gstep, gtap, gcb, gsb, gdl, gsk, gng,
     w_ref, b_ref, sb_ref, dl_ref, sk_ref, ng_ref,
     uin, steps, token_rows, token_cols, upad, zpad, mix, dsl, ddt, drate, small,
-    stage_c, stage_o, stage_s, step_parts, partial, final, relay,
+    stage_c, stage_o, stage_s, step_parts, partial, final, relay, small_out, small_in,
     own_sem, xs_sem, xr_sem, st_sem, conv_sem, gate_sem, next_sem, dstep_sem,
     ps_sem, pr_sem, fin_sem, via_sem, relay_sem, par_sem, plane_sem, world_sem,
+    ship_sem, ship_recv, hand_sem,
 ):
     core = lax.axis_index("ctx")
     sec = lax.axis_index("section")
@@ -272,6 +273,13 @@
     tok = conv_in.shape[2]
     seq = 2 * tok
     other = 1 - core
+    gives = (sec + nsec - 1) // nsec
+    takes = 1 - sec // (nsec - 1)
+    donor = core * gives
+    helper = core * takes
+    own_groups = HALF - donor
+    last = GROUPS - 1
+    halves_of = 4 * HEADS
 
     def place(c, s, d):
         return {"ctx": c, "section": s, "dp": d}
@@ -308,7 +316,7 @@
 
     mine = pl.ds(pl.multiple_of(core * tok, tok), tok)
     theirs = pl.ds(pl.multiple_of(other * tok, tok), tok)
-    own_step = pltpu.make_async_copy(step_in.at[0, 0], steps.at[core], st_sem.at[0])
+    own_step = pltpu.make_async_copy(step_in.at[0, 0], steps.at[0, core], st_sem.at[0])
     own_step.start()
 
     def fetch(j, _):
@@ -322,17 +330,17 @@
     params = [
         pltpu.make_async_copy(src, dst, par_sem.at[at])
         for at, (src, dst) in enumerate((
-            (sb_in, sb_ref), (dl_in, dl_ref), (w_in, w_ref),
-            (b_in, b_ref), (sk_in, sk_ref), (ng_in, ng_ref),
+            (sb_in, sb_ref.at[0]), (dl_in, dl_ref.at[0]), (w_in, w_ref.at[pl.ds(0, 1)]),
+            (b_in, b_ref.at[0]), (sk_in, sk_ref.at[0]), (ng_in, ng_ref.at[0]),
         ))
     ]
     for copy in params:
         copy.start()
-    lax.fori_loop(1, HALF, fetch, 0)
+    lax.fori_loop(1, own_groups, fetch, 0)
     partial[dp] = jnp.zeros(partial.shape[1:], F32)
     upad[0:8, :] = jnp.zeros((8, MIX), F32)
     zpad[seq : seq + 8, :] = jnp.zeros((8, MIX), F32)
-    for ref in (token_rows, ddt, drate, small):
+    for ref in (token_rows, ddt, drate, small, small_out):
         ref[...] = jnp.zeros_like(ref)
 
     @pl.when(sec > 0)
@@ -352,7 +360,7 @@
         pl.semaphore_wait(plane_sem, 1)
 
     step_copy = remote(
-        step_in.at[0, 0], steps.at[core], st_sem.at[1], st_sem.at[2], other, sec, dp
+        step_in.at[0, 0], steps.at[0, core], st_sem.at[1], st_sem.at[2], other, sec, dp
     )
     step_copy.start()
 
@@ -363,21 +371,45 @@
             ).start()
         return 0
 
-    lax.fori_loop(0, HALF, exchange, 0)
+    exchange(0, 0)
+
+    def hand(src, dst, at):
+        return remote(src, dst, ship_sem.at[at], ship_recv.at[at], 1, sec - 1, dp)
+
+    @pl.when(sec > 0)
+    def _():
+        for src, off, width in pieces(last):
+            hand(src, uin.at[HALF, mine, pl.ds(off, width)], 0).start()
+        hand(step_in.at[0, 0], steps.at[1, core], 1).start()
+
+    @pl.when(jnp.logical_and(sec > 0, core == 0))
+    def _():
+        xc, bc, cc = group_columns(last)
+        for col, width in ((xc, WIDE), (bc, STATE), (cc, STATE)):
+            cut = pl.ds(col, width)
+            hand(w_in.at[:, :, cut], w_ref.at[pl.ds(1, 1), :, cut], 2).start()
+            hand(b_in.at[:, cut], b_ref.at[1, :, cut], 3).start()
+        cut = pl.ds(xc, WIDE)
+        hand(ng_in.at[:, cut], ng_ref.at[1, :, cut], 4).start()
+        hand(sb_in, sb_ref.at[1], 5).start()
+        hand(dl_in, dl_ref.at[1], 6).start()
+        hand(sk_in, sk_ref.at[1], 7).start()
+
+    lax.fori_loop(1, HALF - other * gives, exchange, 0)
     for copy in params:
         copy.wait()
 
-    def token_terms():
-        own_step.wait()
-        step_copy.wait()
+    def token_terms(which):
         diagonal = lax.broadcasted_iota(jnp.int32, (HEADS, HEADS), 0) == lax.broadcasted_iota(
             jnp.int32, (HEADS, HEADS), 1
         )
 
         def upright(ref):
-            return jnp.sum(jnp.where(diagonal, ref[...], 0.0), axis=1, keepdims=True)
-
-        raw = jnp.concatenate([steps[0].astype(F32), steps[1].astype(F32)], axis=1)
+            return jnp.sum(jnp.where(diagonal, ref[which], 0.0), axis=1, keepdims=True)
+
+        raw = jnp.concatenate(
+            [steps[which, 0].astype(F32), steps[which, 1].astype(F32)], axis=1
+        )
         raw = raw + upright(sb_ref)
         delta = jnp.maximum(raw, 0.0) + jnp.log1p(jnp.exp(-jnp.abs(raw)))
         rate = delta * (-jnp.exp(upright(dl_ref)))
@@ -387,14 +419,18 @@
         r_hi, r_rest = rate.astype(BF16), rate - rate.astype(BF16).astype(F32)
         r_mid, r_lo = split(r_rest)
         cumulative = dot(r_hi, ones_up, NN) + (dot(r_mid, ones_up, NN) + dot(r_lo, ones_up, NN))
-        token_rows[0:HEADS, :] = delta
-        token_rows[HEADS : 2 * HEADS, :] = cumulative
-        token_rows[2 * HEADS : 3 * HEADS, :] = jax.nn.sigmoid(raw)
-        token_rows[3 * HEADS : 4 * HEADS, :] = rate
+        for at, value in enumerate((delta, cumulative, jax.nn.sigmoid(raw), rate)):
+            top = pl.multiple_of(which * halves_of + at * HEADS, HEADS)
+            token_rows[pl.ds(top, HEADS), :] = value
         token_cols[...] = token_rows[...].T
 
-    def group(j, _):
-        g = core * HALF + j
+    def group(turn, _):
+        j = turn + (turn // (HALF - 1)) * donor
+        helping = j // HALF
+        g = core * HALF + j - helping
+        ours = helping == 0
+        slot_p = j + helping
+        lane0 = helping * halves_of
         cols = group_columns(g)
         blocks = [(0, cols[0])]
         for base, col in ((WIDE, cols[1]), (WIDE + STATE, cols[2])):
@@ -409,21 +445,47 @@
                         j, pl.ds(start, count), here
                     ].astype(F32)
                 window = upad[pl.ds(start, count + 8), here]
-                z = b_ref[:, pl.ds(col, 128)] + w_ref[0, 3:4, pl.ds(col, 128)] * window[8:]
+                z = b_ref[helping, :, pl.ds(col, 128)]
+                z = z + w_ref[helping, 3:4, pl.ds(col, 128)] * window[8:]
                 for k in range(CONV - 1):
-                    z = z + w_ref[0, pl.ds(k, 1), pl.ds(col, 128)] * pltpu.roll(window, 3 - k, 0)[8:]
+                    tap = w_ref[helping, pl.ds(k, 1), pl.ds(col, 128)]
+                    z = z + tap * pltpu.roll(window, 3 - k, 0)[8:]
                 s = jax.nn.sigmoid(z)
                 mix[pl.ds(start, count), here] = z * s
                 dsl[pl.ds(start, count), here] = s * (1.0 + z * (1.0 - s))
 
-        pltpu.make_async_copy(uin.at[j, mine], uin.at[j, mine], own_sem.at[j]).wait()
+        @pl.when(ours)
+        def _():
+            pltpu.make_async_copy(uin.at[j, mine], uin.at[j, mine], own_sem.at[j]).wait()
+
+        @pl.when(helping == 1)
+        def _():
+            some = pl.ds(0, WIDE + 2 * STATE)
+            for at, ref in enumerate((
+                uin.at[HALF], steps.at[1], w_ref.at[pl.ds(1, 1), :, some], b_ref.at[1, :, some],
+                ng_ref.at[1, :, pl.ds(0, WIDE)], sb_ref.at[1], dl_ref.at[1], sk_ref.at[1],
+            )):
+                remote(
+                    ref, ref, ship_sem.at[at], ship_recv.at[at], core, sec + 1, dp
+                ).wait_recv()
+
         conv_rows(pl.multiple_of(core * tok, tok), tok, True)
 
         @pl.when(j == 0)
         def _():
-            token_terms()
-
-        remote(uin.at[j, mine], uin.at[j, theirs], xs_sem.at[j], xr_sem.at[j], other, sec, dp).wait()
+            own_step.wait()
+            step_copy.wait()
+
+        @pl.when(lax.rem(j, HALF) == 0)
+        def _():
+            token_terms(helping)
+
+        @pl.when(ours)
+        def _():
+            remote(
+                uin.at[j, theirs], uin.at[j, theirs], xs_sem.at[j], xr_sem.at[j], other, sec, dp
+            ).wait_recv()
+
         conv_rows(pl.multiple_of(other * tok, tok), tok, True)
         conv_rows(tok, 8, False)
 
@@ -435,10 +497,12 @@
         first = lane < HEAD_DIM
 
         def pick(at):
-            return jnp.sum(jnp.where(lane == at, token_cols[...], 0.0), axis=1, keepdims=True)
+            return jnp.sum(
+                jnp.where(lane == lane0 + at, token_cols[...], 0.0), axis=1, keepdims=True
+            )
 
         def pick1(ref, h):
-            return jnp.sum(jnp.where(lane16 == h, ref[...], 0.0), axis=1, keepdims=True)
+            return jnp.sum(jnp.where(lane16 == h, ref[helping], 0.0), axis=1, keepdims=True)
 
         x = mix[:, 0:WIDE]
         bmap = split(mix[:, WIDE : WIDE + STATE])
@@ -451,7 +515,7 @@
         scores = dot3(cmap, bmap, NT)
         decay, mixed, ys = [], [], []
         for r in range(REPS):
-            seg = pick(HEADS + h0 + r) - token_rows[pl.ds(HEADS + h0 + r, 1), :]
+            seg = pick(HEADS + h0 + r) - token_rows[pl.ds(lane0 + HEADS + h0 + r, 1), :]
             w = jnp.exp(jnp.where(row >= column, seg, -jnp.inf))
             a = scores * w
             a_p = split(a)
@@ -461,7 +525,7 @@
         y = jnp.where(first, ys[0], ys[1]) + skip2 * x
         gate = uin[j, :, MIX : MIX + WIDE].astype(F32)
         cot = uin[j, :, MIX + WIDE : MIX + 2 * WIDE].astype(F32)
-        gain = ng_ref[:, pl.ds(cols[0], WIDE)]
+        gain = ng_ref[helping, :, pl.ds(cols[0], WIDE)]
         s = jax.nn.sigmoid(gate)
         act = gate * s
         gated = y * act
@@ -473,42 +537,53 @@
         dy = dgated * act
         stage_o[j, :, WIDE : 2 * WIDE] = (dgated * y * (s * (1.0 + gate * (1.0 - s)))).astype(BF16)
 
-        odd = lax.rem(j, 2) == 1
+        even = lax.rem(j, 2) == 0
+        out_cut = pl.ds(cols[0], WIDE)
 
         def send_half(base, t, dst, done, landed, s):
             remote(
                 stage_o.at[j, pl.ds(t * tok, tok), pl.ds(base, WIDE)], dst, done, landed, t, s, dp
             ).start()
 
-        @pl.when(jnp.logical_and(sec < nsec - 1, jnp.logical_not(jnp.logical_and(sec == 1, odd))))
+        direct = jnp.logical_and(
+            ours, jnp.logical_and(sec < nsec - 1, jnp.logical_not(jnp.logical_and(sec == 1, even)))
+        )
+
+        @pl.when(direct)
         def _():
             for t in range(2):
-                send_half(
-                    0, t, nxt.at[0, 0, :, pl.ds(cols[0], WIDE)],
-                    next_sem.at[0], next_sem.at[1], sec + 1,
-                )
-
-        @pl.when(jnp.logical_and(sec == 1, odd))
+                send_half(0, t, nxt.at[0, 0, :, out_cut], next_sem.at[0], next_sem.at[1], sec + 1)
+
+        @pl.when(jnp.logical_and(ours, jnp.logical_and(sec == 1, even)))
         def _():
             slot = core * (HALF // 2) + j // 2
             for t in range(2):
                 send_half(0, t, relay.at[slot], next_sem.at[0], relay_sem.at[slot], 3)
 
-        @pl.when(jnp.logical_or(sec == 1, sec == 3))
+        @pl.when(jnp.logical_and(ours, jnp.logical_or(sec == 1, sec == 3)))
         def _():
             for t in range(2):
                 send_half(
-                    WIDE, t, ggate.at[0, 0, :, pl.ds(cols[0], WIDE)],
-                    gate_sem.at[0], gate_sem.at[1], sec - 1,
+                    WIDE, t, ggate.at[0, 0, :, out_cut], gate_sem.at[0], gate_sem.at[1], sec - 1
                 )
 
-        @pl.when(sec == 2)
+        @pl.when(jnp.logical_and(ours, sec == 2))
         def _():
             slot = core * HALF + j
             for t in range(2):
                 send_half(WIDE, t, relay.at[slot], gate_sem.at[0], relay_sem.at[slot], 0)
 
-        partial[dp, j, 5:6, 0:WIDE] = jnp.sum(cot * normed, axis=0, keepdims=True)
+        @pl.when(helping == 1)
+        def _():
+            ggate[0, 0, :, out_cut] = stage_o[j, tok : 2 * tok, WIDE : 2 * WIDE]
+            send_half(WIDE, 0, ggate.at[0, 0, :, out_cut], gate_sem.at[0], gate_sem.at[1], sec)
+
+        @pl.when(jnp.logical_and(helping == 1, sec < nsec - 2))
+        def _():
+            for t in range(2):
+                send_half(0, t, nxt.at[0, 0, :, out_cut], next_sem.at[0], next_sem.at[1], sec + 2)
+
+        partial[dp, slot_p, 5:6, 0:WIDE] = jnp.sum(cot * normed, axis=0, keepdims=True)
         dyx = jnp.sum(dy * x, axis=0, keepdims=True)
         dscore = jnp.zeros((seq, seq), F32)
         dy_p = split(dy)
@@ -527,14 +602,26 @@
                 dz = zpad[0:seq, here]
                 du = jnp.zeros((seq, 128), F32)
                 for k in range(CONV):
-                    du = du + w_ref[0, pl.ds(k, 1), pl.ds(col, 128)] * zpad[3 - k : 3 - k + seq, here]
-                    partial[dp, j, pl.ds(k, 1), here] = jnp.sum(
+                    du = du + (
+                        w_ref[helping, pl.ds(k, 1), pl.ds(col, 128)]
+                        * zpad[3 - k : 3 - k + seq, here]
+                    )
+                    partial[dp, slot_p, pl.ds(k, 1), here] = jnp.sum(
                         dz * upad[5 + k : 5 + k + seq, here], axis=0, keepdims=True
                     )
-                partial[dp, j, pl.ds(4, 1), here] = jnp.sum(dz, axis=0, keepdims=True)
+                partial[dp, slot_p, pl.ds(4, 1), here] = jnp.sum(dz, axis=0, keepdims=True)
                 stage_c[j, :, here] = du.astype(BF16)
 
-            @pl.when(sec > 0)
+            @pl.when(helping == 1)
+            def _():
+                gconv[0, 0, :, pl.ds(start, width)] = stage_c[j, tok : 2 * tok, off : off + width]
+                remote(
+                    stage_c.at[j, pl.ds(0, tok), pl.ds(off, width)],
+                    gconv.at[0, 0, :, pl.ds(start, width)],
+                    conv_sem.at[0], conv_sem.at[1], 0, sec, dp,
+                ).start()
+
+            @pl.when(jnp.logical_and(ours, sec > 0))
             def _():
                 for t in range(2):
                     remote(
@@ -557,11 +644,11 @@
             p = split(das[r] * mixed[r][0])
             later = dot(upper, p[0], NN) + dot(upper, p[1], NN)
             dr = jnp.sum(jnp.where(row > column, later, 0.0), axis=1, keepdims=True)
-            drate[...] += jnp.where(lane == h0 + r, dr, 0.0)
+            drate[...] += jnp.where(lane == lane0 + h0 + r, dr, 0.0)
             total = jnp.sum(jnp.where(own[0:1], dyx, 0.0), axis=1, keepdims=True)
-            small[2:3, :] += jnp.where(lane1 == h0 + r, total, 0.0)
+            small[2:3, :] += jnp.where(lane1 == lane0 + h0 + r, total, 0.0)
             dd = jnp.sum(jnp.where(own, dxx, 0.0), axis=1, keepdims=True)
-            ddt[...] += jnp.where(lane == h0 + r, dd, 0.0)
+            ddt[...] += jnp.where(lane == lane0 + h0 + r, dd, 0.0)
 
         @pl.when(jnp.logical_and(j == 0, sec == 0))
         def _():
@@ -575,14 +662,28 @@
         def _():
             pl.semaphore_wait(world_sem, 1)
 
+        @pl.when(ours)
+        def _():
+            spread(j)
+
+        @pl.when(helping == 1)
+        def _():
+            remote(
+                partial.at[dp, HALF + 1], partial.at[dp, HALF - 1],
+                hand_sem.at[0], hand_sem.at[1], core, sec + 1, dp,
+            ).start()
+
+        return 0
+
+    def spread(slot):
         for k in range(1, ndp):
             to = lax.rem(dp + k, ndp)
             remote(
-                partial.at[dp, j], partial.at[dp, j], ps_sem.at[to], pr_sem.at[dp], core, sec, to
+                partial.at[dp, slot], partial.at[dp, slot], ps_sem.at[to], pr_sem.at[dp],
+                core, sec, to,
             ).start()
-        return 0
-
-    lax.fori_loop(0, HALF, group, 0)
+
+    lax.fori_loop(0, own_groups + helper, group, 0)
 
     def pass_on(slot, g, out, landed, s):
         part = relay.at[slot]
@@ -593,13 +694,13 @@
 
     @pl.when(sec == 0)
     def _():
-        for g in range(GROUPS):
+        for g in range(GROUPS - 1):
             pass_on(g, g, ggate, gate_sem.at[1], 1)
 
     @pl.when(sec == 3)
     def _():
         for at in range(GROUPS // 2):
-            pass_on(at, 2 * at + 1, nxt, next_sem.at[1], 2)
+            pass_on(at, 2 * at, nxt, next_sem.at[1], 2)
 
     @pl.when(sec == 0)
     def _():
@@ -611,14 +712,27 @@
         ggate[...] = jnp.zeros_like(ggate)
         gstep[...] = jnp.zeros_like(gstep)
 
-    damp = jnp.exp(dl_ref[...])
-    dr16 = drate[:, 0:HEADS]
-    dstep = (ddt[:, 0:HEADS] - dr16 * damp) * token_cols[:, 2 * HEADS : 3 * HEADS]
-    small[0:1, 0:HEADS] = jnp.sum(dstep, axis=0, keepdims=True)
-    small[1:2, 0:HEADS] = jnp.sum(
-        dr16 * token_cols[:, 3 * HEADS : 4 * HEADS], axis=0, keepdims=True
-    )
-    drate[:, 0:HEADS] = dstep
+    def step_terms(which, into):
+        lane0 = which * halves_of
+        heads = slice(lane0, lane0 + HEADS)
+        dr16 = drate[:, heads]
+        gate = token_cols[:, lane0 + 2 * HEADS : lane0 + 3 * HEADS]
+        rate = token_cols[:, lane0 + 3 * HEADS : lane0 + 4 * HEADS]
+        dstep = (ddt[:, heads] - dr16 * jnp.exp(dl_ref[which])) * gate
+        into[0:1, 0:HEADS] = jnp.sum(dstep, axis=0, keepdims=True)
+        into[1:2, 0:HEADS] = jnp.sum(dr16 * rate, axis=0, keepdims=True)
+        drate[:, heads] = dstep
+
+    step_terms(0, small)
+
+    @pl.when(helper == 1)
+    def _():
+        step_terms(1, small_out)
+        small_out[2:3, 0:HEADS] = small[2:3, halves_of : halves_of + HEADS]
+        remote(
+            small_out, small_in, hand_sem.at[2], hand_sem.at[3], core, sec + 1, dp
+        ).start()
+
     turned = drate[...].T
     for t in range(2):
         stage_s[t] = turned[0:HEADS, t * tok : (t + 1) * tok].astype(BF16)
@@ -631,18 +745,33 @@
                 dstep_sem.at[2], dstep_sem.at[core], t, sec - 1, dp,
             ).start()
 
+    @pl.when(helper == 1)
+    def _():
+        stage_s[2] = turned[halves_of : halves_of + HEADS, 0:tok].astype(BF16)
+        step_parts[2] = turned[halves_of : halves_of + HEADS, tok : 2 * tok].astype(BF16)
+        remote(
+            stage_s.at[2], step_parts.at[2], dstep_sem.at[4], dstep_sem.at[3], other, sec, dp
+        ).start()
+
+    @pl.when(donor == 1)
+    def _():
+        landed = partial.at[dp, HALF - 1]
+        remote(landed, landed, hand_sem.at[0], hand_sem.at[1], core, sec - 1, dp).wait_recv()
+        spread(HALF - 1)
+        remote(small_in, small_in, hand_sem.at[2], hand_sem.at[3], core, sec - 1, dp).wait_recv()
+        small[...] += small_in[...]
+
     partial[dp, HALF, :, 0:128] = small[...]
+    spread(HALF)
     for k in range(1, ndp):
         to = lax.rem(dp + k, ndp)
         remote(
-            partial.at[dp, HALF], partial.at[dp, HALF], ps_sem.at[to], pr_sem.at[dp], core, sec, to
-        ).start()
+            partial.at[dp, pl.ds(0, HALF + 1)], partial.at[to, pl.ds(0, HALF + 1)],
+            ps_sem.at[to], pr_sem.at[to], core, sec, to,
+        ).wait()
+    total = partial[0, 0 : HALF + 1]
     for k in range(1, ndp):
-        to = lax.rem(dp + k, ndp)
-        remote(partial.at[dp], partial.at[to], ps_sem.at[to], pr_sem.at[to], core, sec, to).wait()
-    total = partial[0]
-    for k in range(1, ndp):
-        total = total + partial[k]
+        total = total + partial[k, 0 : HALF + 1]
     final[core] = total
     halves = remote(final.at[core], final.at[core], fin_sem.at[0], fin_sem.at[1], other, sec, dp)
     halves.start()
@@ -665,37 +794,84 @@
         for c in range(2):
             part = step_parts.at[c]
             remote(part, part, dstep_sem.at[2], dstep_sem.at[c], core, sec + 1, dp).wait_recv()
-        gstep[0, 0] = (step_parts[0].astype(F32) + step_parts[1].astype(F32)).astype(BF16)
+
+        @pl.when(core == 0)
+        def _():
+            part = step_parts.at[2]
+            remote(part, part, dstep_sem.at[4], dstep_sem.at[3], other, sec, dp).wait_recv()
+
+        both = step_parts[0].astype(F32) + step_parts[1].astype(F32)
+        gstep[0, 0] = (both + step_parts[2].astype(F32)).astype(BF16)
+
+    def sent(ref, sem):
+        remote(ref, ref, sem, sem, other, sec, dp).wait_send()
+
+    def landed(ref, sem):
+        remote(ref, ref, sem, sem, other, sec, dp).wait_recv()
+
+    def exchanged(j, _):
+        sent(uin.at[j, mine], xs_sem.at[j])
+        return 0
+
+    lax.fori_loop(0, HALF - other * gives, exchanged, 0)
+    first = pl.ds(0, HALF - 1)
+    half = pl.ds(0, WIDE)
 
     @pl.when(sec == 0)
     def _():
-        remote(relay, relay, via_sem.at[0], relay_sem.at[0], core, 1, dp).wait_send()
+        sent(relay.at[pl.ds(0, GROUPS - 1)], via_sem.at[0])
+
+    @pl.when(sec == nsec - 1)
+    def _():
+        sent(relay.at[pl.ds(0, GROUPS // 2)], via_sem.at[0])
 
     @pl.when(sec > 0)
     def _():
-        low = sec - 1
-        remote(stage_c, stage_c, conv_sem.at[0], conv_sem.at[1], core, low, dp).wait_send()
-        half_o = stage_o.at[:, :, pl.ds(0, WIDE)]
-        remote(half_o, half_o, gate_sem.at[0], gate_sem.at[1], core, low, dp).wait_send()
-        remote(stage_s, stage_s, dstep_sem.at[2], dstep_sem.at[0], core, low, dp).wait_send()
-        remote(
-            nxt.at[0, 0], nxt.at[0, 0], next_sem.at[0], next_sem.at[1], core, low, dp
-        ).wait_recv()
-
-    @pl.when(sec == nsec - 1)
-    def _():
-        used = relay.at[pl.ds(0, GROUPS // 2)]
-        remote(used, used, via_sem.at[0], relay_sem.at[0], core, 2, dp).wait_send()
+        sent(uin.at[HALF, pl.ds(0, tok)], ship_sem.at[0])
+        sent(steps.at[1, 0], ship_sem.at[1])
+        sent(stage_c.at[first], conv_sem.at[0])
+        sent(stage_o.at[first, :, half], gate_sem.at[0])
+        sent(stage_s.at[pl.ds(0, 2)], dstep_sem.at[2])
+        landed(nxt.at[0, 0], next_sem.at[1])
+
+    @pl.when(jnp.logical_and(sec > 0, core == 0))
+    def _():
+        some = pl.ds(0, WIDE + 2 * STATE)
+        sent(w_ref.at[pl.ds(1, 1), :, some], ship_sem.at[2])
+        sent(b_ref.at[1, :, some], ship_sem.at[3])
+        sent(ng_ref.at[1, :, half], ship_sem.at[4])
+        sent(sb_ref.at[1], ship_sem.at[5])
+        sent(dl_ref.at[1], ship_sem.at[6])
+        sent(sk_ref.at[1], ship_sem.at[7])
+        sent(stage_c.at[HALF - 1], conv_sem.at[0])
+        sent(stage_o.at[HALF - 1, :, half], gate_sem.at[0])
 
     @pl.when(sec < nsec - 1)
     def _():
-        high = sec + 1
-        half_o = stage_o.at[:, :, pl.ds(0, WIDE)]
-        remote(half_o, half_o, next_sem.at[0], next_sem.at[1], core, high, dp).wait_send()
-        whole = ggate.at[0, 0]
-        remote(whole, whole, gate_sem.at[0], gate_sem.at[1], core, high, dp).wait_recv()
-        whole = gconv.at[0, 0]
-        remote(whole, whole, conv_sem.at[0], conv_sem.at[1], core, high, dp).wait_recv()
+        sent(stage_o.at[first, :, half], next_sem.at[0])
+
+    @pl.when(jnp.logical_and(sec < nsec - 1, donor == 0))
+    def _():
+        sent(stage_o.at[HALF - 1, :, half], next_sem.at[0])
+
+    @pl.when(helper == 1)
+    def _():
+        sent(stage_c.at[HALF, pl.ds(0, tok)], conv_sem.at[0])
+        sent(stage_o.at[HALF, pl.ds(0, tok), half], gate_sem.at[0])
+        sent(stage_s.at[2], dstep_sem.at[4])
+        sent(partial.at[dp, HALF + 1], hand_sem.at[0])
+        sent(small_out, hand_sem.at[2])
+        landed(ggate.at[0, 0, :, pl.ds(0, INNER - WIDE)], gate_sem.at[1])
+        landed(gconv.at[0, 0, :, pl.ds(0, (GROUPS - 1) * MIX)], conv_sem.at[1])
+
+    @pl.when(jnp.logical_and(helper == 1, sec < nsec - 2))
+    def _():
+        sent(stage_o.at[HALF, :, half], next_sem.at[0])
+
+    @pl.when(jnp.logical_and(sec < nsec - 1, core == 0))
+    def _():
+        landed(ggate.at[0, 0], gate_sem.at[1])
+        landed(gconv.at[0, 0], conv_sem.at[1])
 
 
 def finish_kernel(*refs):
@@ -718,14 +894,14 @@
     hbm = pl.BlockSpec(memory_space=pl.ANY)
     vmem = pl.BlockSpec(memory_space=pltpu.VMEM)
     scratch = [
-        pltpu.VMEM(conv_weight.shape, F32),
-        pltpu.VMEM(conv_bias.shape, F32),
-        pltpu.VMEM(step_bias.shape, F32),
-        pltpu.VMEM(decay_log.shape, F32),
-        pltpu.VMEM(skip_gain.shape, F32),
-        pltpu.VMEM(norm_gain.shape, F32),
-        pltpu.VMEM((HALF, seq, MIX + 2 * WIDE), BF16),
-        pltpu.VMEM((2, HEADS, tok), BF16),
+        pltpu.VMEM((2,) + conv_weight.shape[1:], F32),
+        pltpu.VMEM((2,) + conv_bias.shape, F32),
+        pltpu.VMEM((2,) + step_bias.shape, F32),
+        pltpu.VMEM((2,) + decay_log.shape, F32),
+        pltpu.VMEM((2,) + skip_gain.shape, F32),
+        pltpu.VMEM((2,) + norm_gain.shape, F32),
+        pltpu.VMEM((HALF + 1, seq, MIX + 2 * WIDE), BF16),
+        pltpu.VMEM((2, 2, HEADS, tok), BF16),
         pltpu.VMEM((128, seq), F32),
         pltpu.VMEM((seq, 128), F32),
         pltpu.VMEM((seq + 8, MIX), F32),
@@ -735,13 +911,15 @@
         pltpu.VMEM((seq, 128), F32),
         pltpu.VMEM((seq, 128), F32),
         pltpu.VMEM((8, 128), F32),
-        pltpu.VMEM((HALF, seq, MIX), BF16),
-        pltpu.VMEM((HALF, seq, 2 * WIDE), BF16),
-        pltpu.VMEM((2, HEADS, tok), BF16),
-        pltpu.VMEM((2, HEADS, tok), BF16),
-        pltpu.VMEM((ndp, HALF + 1, 8, MIX), F32),
+        pltpu.VMEM((HALF + 1, seq, MIX), BF16),
+        pltpu.VMEM((HALF + 1, seq, 2 * WIDE), BF16),
+        pltpu.VMEM((3, HEADS, tok), BF16),
+        pltpu.VMEM((3, HEADS, tok), BF16),
+        pltpu.VMEM((ndp, HALF + 2, 8, MIX), F32),
         pltpu.VMEM((2, HALF + 1, 8, MIX), F32),
         pltpu.VMEM((GROUPS, tok, WIDE), BF16),
+        pltpu.VMEM((8, 128), F32),
+        pltpu.VMEM((8, 128), F32),
         pltpu.SemaphoreType.DMA((HALF,)),
         pltpu.SemaphoreType.DMA((HALF,)),
         pltpu.SemaphoreType.DMA((HALF,)),
@@ -749,7 +927,7 @@
         pltpu.SemaphoreType.DMA((2,)),
         pltpu.SemaphoreType.DMA((2,)),
         pltpu.SemaphoreType.DMA((2,)),
-        pltpu.SemaphoreType.DMA((3,)),
+        pltpu.SemaphoreType.DMA((5,)),
         pltpu.SemaphoreType.DMA((ndp,)),
         pltpu.SemaphoreType.DMA((ndp,)),
         pltpu.SemaphoreType.DMA((2,)),
@@ -758,6 +936,9 @@
         pltpu.SemaphoreType.DMA((6,)),
         pltpu.SemaphoreType.REGULAR,
         pltpu.SemaphoreType.REGULAR,
+        pltpu.SemaphoreType.DMA((8,)),
+        pltpu.SemaphoreType.DMA((8,)),
+        pltpu.SemaphoreType.DMA((4,)),
     ]
     turned = jnp.swapaxes(step_input, 2, 3)
     shapes = [

time: 47.6 us -> 45.7 us (0.960)
  Pallas kernels: 46.8 us -> 44.9 us
    pallas_call x1, Pallas kernels: 45.4 us -> 43.6 us  [paired(): pl.pallas_call(pair_kernel, name='mixer_tick', in_specs=[hbm] * 10, out_s...]
where the time goes in v3:
time: 45.7 us; the launch traced here: 45.6 us
  Pallas kernels  44.9 us (98%)
  between operations  0.65 us (1%)
    pallas_call x1, Pallas kernels, paired(): pl.pallas_call(pair_kernel, name='mixer_tick', in_specs=[hbm] * 10, out_s...  43.6 us
    pallas_call x1, Pallas kernels, paired(): pl.pallas_call(finish_kernel, name='mixer_finish', in_specs=[vmem] * 10,...  1.35 us

profile of v3, /device:TPU:0, one launch (start us, length us, event | category | flops | bytes accessed | tf_op | source)
XLA Modules:
  0.0 45.6 jit_solution(12649088261871355598)
XLA Ops:
  0.6 43.6 %mixer_tick.1 = (bf16[1,1,128,1024]{3,2,1,0:T(8,128)(2,1)S(1)}, bf16[1,1,128,5120]{3,2,1,0:T(8,128)(2,1)S(1)}, bf16[1,1,128,1024]{3,2,1,0:T(8,128)(2,1)S(1)}, bf...) custom-call(bf16[1,1,128,5120]{3,2,1,0:T(8,128)(2,1)} %conv_in.1, ...), custom_call_target="tpu_custom_call" | custom-call | tf_op jit(solution)/shard_map/mixer_tick/pallas_call | solution.py:963
  44.2 1.3 %mixer_finish.1 = (bf16[1,1,128,1024]{3,2,1,0:T(8,128)(2,1)}, bf16[1,1,128,5120]{3,2,1,0:T(8,128)(2,1)}, bf16[1,1,128,1024]{3,2,1,0:T(8,128)(2,1)}, bf16[1,1,16,...) custom-call(bf16[1,1,128,1024]{3,2,1,0:T(8,128)(2,1)S(1)} %get-tuple, ...), custom_call_target="tpu_custom_call" | custom-call | tf_op jit(solution)/shard_map/mixer_finish/pallas_call | solution.py:974

commit v4 on v3

--- a/solution.py
+++ b/solution.py
@@ -262,7 +262,7 @@
     uin, steps, token_rows, token_cols, upad, zpad, mix, dsl, ddt, drate, small,
     stage_c, stage_o, stage_s, step_parts, partial, final, relay, small_out, small_in,
     own_sem, xs_sem, xr_sem, st_sem, conv_sem, gate_sem, next_sem, dstep_sem,
-    ps_sem, pr_sem, fin_sem, via_sem, relay_sem, par_sem, plane_sem, world_sem,
+    ps_sem, pr_sem, fin_sem, via_sem, relay_sem, par_sem, pair_sem, plane_sem, world_sem,
     ship_sem, ship_recv, hand_sem,
 ):
     core = lax.axis_index("ctx")
@@ -298,9 +298,9 @@
         pl.semaphore_signal(barrier, inc=1, device_id=place(c, s, d), device_id_type=MESH)
 
     for c in range(2):
-        for s in range(1, 4):
-
-            @pl.when(jnp.logical_or(sec != s, core != c))
+        for s in (1, 3):
+
+            @pl.when(jnp.logical_and(sec // 2 == s // 2, jnp.logical_or(sec != s, core != c)))
             def _():
                 greet(c, s, dp)
 
@@ -343,47 +343,24 @@
     for ref in (token_rows, ddt, drate, small, small_out):
         ref[...] = jnp.zeros_like(ref)
 
-    @pl.when(sec > 0)
-    def _():
-        pl.semaphore_wait(barrier, 7)
-
-    @pl.when(sec == 1)
-    def _():
-        pl.semaphore_signal(
-            plane_sem, inc=1, device_id=place(core, 0, dp), device_id_type=MESH
-        )
-        for k in range(1, ndp):
-            greet(core, 0, lax.rem(dp + k, ndp))
-
-    @pl.when(sec == 0)
-    def _():
-        pl.semaphore_wait(plane_sem, 1)
-
-    step_copy = remote(
-        step_in.at[0, 0], steps.at[0, core], st_sem.at[1], st_sem.at[2], other, sec, dp
-    )
-    step_copy.start()
-
-    def exchange(j, _):
-        for src, off, width in pieces(other * HALF + j):
-            remote(
-                src, uin.at[j, mine, pl.ds(off, width)], xs_sem.at[j], xr_sem.at[j], other, sec, dp
-            ).start()
-        return 0
-
-    exchange(0, 0)
+    upper = lax.rem(sec, 2) == 1
+
+    def tell(sem, s):
+        pl.semaphore_signal(sem, inc=1, device_id=place(core, s, dp), device_id_type=MESH)
+
+    @pl.when(upper)
+    def _():
+        pl.semaphore_wait(barrier, 3)
 
     def hand(src, dst, at):
         return remote(src, dst, ship_sem.at[at], ship_recv.at[at], 1, sec - 1, dp)
 
-    @pl.when(sec > 0)
-    def _():
+    def hand_over():
         for src, off, width in pieces(last):
             hand(src, uin.at[HALF, mine, pl.ds(off, width)], 0).start()
         hand(step_in.at[0, 0], steps.at[1, core], 1).start()
 
-    @pl.when(jnp.logical_and(sec > 0, core == 0))
-    def _():
+    def hand_params():
         xc, bc, cc = group_columns(last)
         for col, width in ((xc, WIDE), (bc, STATE), (cc, STATE)):
             cut = pl.ds(col, width)
@@ -394,6 +371,44 @@
         hand(sb_in, sb_ref.at[1], 5).start()
         hand(dl_in, dl_ref.at[1], 6).start()
         hand(sk_in, sk_ref.at[1], 7).start()
+
+    @pl.when(upper)
+    def _():
+        tell(pair_sem, sec - 1)
+        hand_over()
+
+    @pl.when(sec == 1)
+    def _():
+        greet(core, 2, dp)
+
+    @pl.when(jnp.logical_not(upper))
+    def _():
+        pl.semaphore_wait(pair_sem, 1)
+
+    step_copy = remote(
+        step_in.at[0, 0], steps.at[0, core], st_sem.at[1], st_sem.at[2], other, sec, dp
+    )
+    step_copy.start()
+
+    def exchange(j, _):
+        for src, off, width in pieces(other * HALF + j):
+            remote(
+                src, uin.at[j, mine, pl.ds(off, width)], xs_sem.at[j], xr_sem.at[j], other, sec, dp
+            ).start()
+        return 0
+
+    exchange(0, 0)
+
+    @pl.when(sec == 2)
+    def _():
+        pl.semaphore_wait(barrier, 1)
+        tell(plane_sem, 0)
+        tell(plane_sem, 1)
+        hand_over()
+
+    @pl.when(jnp.logical_and(sec > 0, core == 0))
+    def _():
+        hand_params()
 
     lax.fori_loop(1, HALF - other * gives, exchange, 0)
     for copy in params:
@@ -475,6 +490,12 @@
         def _():
             own_step.wait()
             step_copy.wait()
+
+        @pl.when(jnp.logical_and(j == 0, sec == 1))
+        def _():
+            pl.semaphore_wait(plane_sem, 1)
+            for k in range(1, ndp):
+                greet(core, 0, lax.rem(dp + k, ndp))
 
         @pl.when(lax.rem(j, HALF) == 0)
         def _():
@@ -652,6 +673,7 @@
 
         @pl.when(jnp.logical_and(j == 0, sec == 0))
         def _():
+            pl.semaphore_wait(plane_sem, 1)
             pl.semaphore_wait(barrier, ndp - 1)
             for s in range(1, 4):
                 pl.semaphore_signal(
@@ -936,6 +958,7 @@
         pltpu.SemaphoreType.DMA((6,)),
         pltpu.SemaphoreType.REGULAR,
         pltpu.SemaphoreType.REGULAR,
+        pltpu.SemaphoreType.REGULAR,
         pltpu.SemaphoreType.DMA((8,)),
         pltpu.SemaphoreType.DMA((8,)),
         pltpu.SemaphoreType.DMA((4,)),

time: 45.7 us -> 44.6 us (0.976)
  Pallas kernels: 44.9 us -> 43.8 us
    pallas_call x1, Pallas kernels: 43.6 us -> 42.5 us  [paired(): pl.pallas_call(pair_kernel, name='mixer_tick', in_specs=[hbm] * 10, out_s...]
where the time goes in v4:
time: 44.6 us; the launch traced here: 44.5 us
  Pallas kernels  43.8 us (98%)
  between operations  0.65 us (1%)
    pallas_call x1, Pallas kernels, paired(): pl.pallas_call(pair_kernel, name='mixer_tick', in_specs=[hbm] * 10, out_s...  42.5 us
    pallas_call x1, Pallas kernels, paired(): pl.pallas_call(finish_kernel, name='mixer_finish', in_specs=[vmem] * 10,...  1.35 us

profile of v4, /device:TPU:0, one launch (start us, length us, event | category | flops | bytes accessed | tf_op | source)
XLA Modules:
  0.0 44.5 jit_solution(13870258512653937143)
XLA Ops:
  0.6 42.5 %mixer_tick.1 = (bf16[1,1,128,1024]{3,2,1,0:T(8,128)(2,1)S(1)}, bf16[1,1,128,5120]{3,2,1,0:T(8,128)(2,1)S(1)}, bf16[1,1,128,1024]{3,2,1,0:T(8,128)(2,1)S(1)}, bf...) custom-call(bf16[1,1,128,5120]{3,2,1,0:T(8,128)(2,1)} %conv_in.1, ...), custom_call_target="tpu_custom_call" | custom-call | tf_op jit(solution)/shard_map/mixer_tick/pallas_call | solution.py:986
  43.1 1.3 %mixer_finish.1 = (bf16[1,1,128,1024]{3,2,1,0:T(8,128)(2,1)}, bf16[1,1,128,5120]{3,2,1,0:T(8,128)(2,1)}, bf16[1,1,128,1024]{3,2,1,0:T(8,128)(2,1)}, bf16[1,1,16,...) custom-call(bf16[1,1,128,1024]{3,2,1,0:T(8,128)(2,1)S(1)} %get-tuple, ...), custom_call_target="tpu_custom_call" | custom-call | tf_op jit(solution)/shard_map/mixer_finish/pallas_call | solution.py:997

commit v5 on v4

--- a/solution.py
+++ b/solution.py
@@ -258,12 +258,11 @@
 def pair_kernel(
     conv_in, gate_in, step_in, cot_in, w_in, b_in, sb_in, dl_in, sk_in, ng_in,
     nxt, gconv, ggate, gstep, gtap, gcb, gsb, gdl, gsk, gng,
-    w_ref, b_ref, sb_ref, dl_ref, sk_ref, ng_ref,
+    w_ref, b_ref, per_head, ng_ref,
     uin, steps, token_rows, token_cols, upad, zpad, mix, dsl, ddt, drate, small,
     stage_c, stage_o, stage_s, step_parts, partial, final, relay, small_out, small_in,
-    own_sem, xs_sem, xr_sem, st_sem, conv_sem, gate_sem, next_sem, dstep_sem,
-    ps_sem, pr_sem, fin_sem, via_sem, relay_sem, par_sem, pair_sem, plane_sem, world_sem,
-    ship_sem, ship_recv, hand_sem,
+    own_sem, xr_sem, sent_sem, land_sem, load_sem, step_sem, ship_sem, relay_sem, dstep_sem,
+    sum_sem, hand_sem, fin_sem, pair_sem, plane_sem, world_sem,
 ):
     core = lax.axis_index("ctx")
     sec = lax.axis_index("section")
@@ -284,14 +283,15 @@
     def place(c, s, d):
         return {"ctx": c, "section": s, "dp": d}
 
-    def remote(src, dst, send, recv, c, s, d):
+    def remote(src, dst, recv, c, s, d):
         return pltpu.make_async_remote_copy(
-            src_ref=src, dst_ref=dst, send_sem=send, recv_sem=recv,
+            src_ref=src, dst_ref=dst, send_sem=sent_sem, recv_sem=recv,
             device_id=place(c, s, d), device_id_type=MESH,
         )
 
     after = lax.rem(sec + 1, nsec)
     before = lax.rem(sec + nsec - 1, nsec)
+    sb_ref, dl_ref, sk_ref = (per_head.at[:, at] for at in range(3))
     barrier = pltpu.get_barrier_semaphore()
 
     def greet(c, s, d):
@@ -316,33 +316,6 @@
 
     mine = pl.ds(pl.multiple_of(core * tok, tok), tok)
     theirs = pl.ds(pl.multiple_of(other * tok, tok), tok)
-    own_step = pltpu.make_async_copy(step_in.at[0, 0], steps.at[0, core], st_sem.at[0])
-    own_step.start()
-
-    def fetch(j, _):
-        for src, off, width in pieces(core * HALF + j):
-            pltpu.make_async_copy(
-                src, uin.at[j, mine, pl.ds(off, width)], own_sem.at[j]
-            ).start()
-        return 0
-
-    fetch(0, 0)
-    params = [
-        pltpu.make_async_copy(src, dst, par_sem.at[at])
-        for at, (src, dst) in enumerate((
-            (sb_in, sb_ref.at[0]), (dl_in, dl_ref.at[0]), (w_in, w_ref.at[pl.ds(0, 1)]),
-            (b_in, b_ref.at[0]), (sk_in, sk_ref.at[0]), (ng_in, ng_ref.at[0]),
-        ))
-    ]
-    for copy in params:
-        copy.start()
-    lax.fori_loop(1, own_groups, fetch, 0)
-    partial[dp] = jnp.zeros(partial.shape[1:], F32)
-    upad[0:8, :] = jnp.zeros((8, MIX), F32)
-    zpad[seq : seq + 8, :] = jnp.zeros((8, MIX), F32)
-    for ref in (token_rows, ddt, drate, small, small_out):
-        ref[...] = jnp.zeros_like(ref)
-
     upper = lax.rem(sec, 2) == 1
 
     def tell(sem, s):
@@ -352,8 +325,14 @@
     def _():
         pl.semaphore_wait(barrier, 3)
 
+    def landed(ref, sem):
+        remote(ref, ref, sem, other, sec, dp).wait_recv()
+
+    def sent(ref):
+        remote(ref, ref, sent_sem, other, sec, dp).wait_send()
+
     def hand(src, dst, at):
-        return remote(src, dst, ship_sem.at[at], ship_recv.at[at], 1, sec - 1, dp)
+        return remote(src, dst, ship_sem.at[at], 1, sec - 1, dp)
 
     def hand_over():
         for src, off, width in pieces(last):
@@ -369,8 +348,8 @@
         cut = pl.ds(xc, WIDE)
         hand(ng_in.at[:, cut], ng_ref.at[1, :, cut], 4).start()
         hand(sb_in, sb_ref.at[1], 5).start()
-        hand(dl_in, dl_ref.at[1], 6).start()
-        hand(sk_in, sk_ref.at[1], 7).start()
+        hand(dl_in, dl_ref.at[1], 5).start()
+        hand(sk_in, sk_ref.at[1], 5).start()
 
     @pl.when(upper)
     def _():
@@ -381,19 +360,42 @@
     def _():
         greet(core, 2, dp)
 
+    own_step = pltpu.make_async_copy(step_in.at[0, 0], steps.at[0, core], load_sem.at[0])
+    own_step.start()
+
+    def fetch(j, _):
+        for src, off, width in pieces(core * HALF + j):
+            pltpu.make_async_copy(
+                src, uin.at[j, mine, pl.ds(off, width)], own_sem.at[j]
+            ).start()
+        return 0
+
+    fetch(0, 0)
+    params = [
+        pltpu.make_async_copy(src, dst, load_sem.at[at])
+        for src, dst, at in (
+            (sb_in, sb_ref.at[0], 1), (dl_in, dl_ref.at[0], 1), (sk_in, sk_ref.at[0], 1),
+            (w_in, w_ref.at[pl.ds(0, 1)], 2), (b_in, b_ref.at[0], 3), (ng_in, ng_ref.at[0], 4),
+        )
+    ]
+    for copy in params:
+        copy.start()
+    lax.fori_loop(1, own_groups, fetch, 0)
+    upad[0:8, :] = jnp.zeros((8, MIX), F32)
+    zpad[seq : seq + 8, :] = jnp.zeros((8, MIX), F32)
+    for ref in (token_rows, ddt, drate, small, small_out):
+        ref[...] = jnp.zeros_like(ref)
+
     @pl.when(jnp.logical_not(upper))
     def _():
         pl.semaphore_wait(pair_sem, 1)
 
-    step_copy = remote(
-        step_in.at[0, 0], steps.at[0, core], st_sem.at[1], st_sem.at[2], other, sec, dp
-    )
-    step_copy.start()
+    remote(step_in.at[0, 0], steps.at[0, core], step_sem, other, sec, dp).start()
 
     def exchange(j, _):
         for src, off, width in pieces(other * HALF + j):
             remote(
-                src, uin.at[j, mine, pl.ds(off, width)], xs_sem.at[j], xr_sem.at[j], other, sec, dp
+                src, uin.at[j, mine, pl.ds(off, width)], xr_sem.at[j], other, sec, dp
             ).start()
         return 0
 
@@ -411,7 +413,9 @@
         hand_params()
 
     lax.fori_loop(1, HALF - other * gives, exchange, 0)
-    for copy in params:
+    own_step.wait()
+    pltpu.make_async_copy(per_head.at[0], per_head.at[0], load_sem.at[1]).wait()
+    for copy in params[3:]:
         copy.wait()
 
     def token_terms(which):
@@ -478,18 +482,15 @@
             some = pl.ds(0, WIDE + 2 * STATE)
             for at, ref in enumerate((
                 uin.at[HALF], steps.at[1], w_ref.at[pl.ds(1, 1), :, some], b_ref.at[1, :, some],
-                ng_ref.at[1, :, pl.ds(0, WIDE)], sb_ref.at[1], dl_ref.at[1], sk_ref.at[1],
+                ng_ref.at[1, :, pl.ds(0, WIDE)], per_head.at[1],
             )):
-                remote(
-                    ref, ref, ship_sem.at[at], ship_recv.at[at], core, sec + 1, dp
-                ).wait_recv()
+                landed(ref, ship_sem.at[at])
 
         conv_rows(pl.multiple_of(core * tok, tok), tok, True)
 
         @pl.when(j == 0)
         def _():
-            own_step.wait()
-            step_copy.wait()
+            landed(steps.at[0, other], step_sem)
 
         @pl.when(jnp.logical_and(j == 0, sec == 1))
         def _():
@@ -503,9 +504,7 @@
 
         @pl.when(ours)
         def _():
-            remote(
-                uin.at[j, theirs], uin.at[j, theirs], xs_sem.at[j], xr_sem.at[j], other, sec, dp
-            ).wait_recv()
+            landed(uin.at[j, theirs], xr_sem.at[j])
 
         conv_rows(pl.multiple_of(other * tok, tok), tok, True)
         conv_rows(tok, 8, False)
@@ -561,9 +560,9 @@
         even = lax.rem(j, 2) == 0
         out_cut = pl.ds(cols[0], WIDE)
 
-        def send_half(base, t, dst, done, landed, s):
+        def send_half(base, t, dst, sem, s):
             remote(
-                stage_o.at[j, pl.ds(t * tok, tok), pl.ds(base, WIDE)], dst, done, landed, t, s, dp
+                stage_o.at[j, pl.ds(t * tok, tok), pl.ds(base, WIDE)], dst, sem, t, s, dp
             ).start()
 
         direct = jnp.logical_and(
@@ -573,37 +572,39 @@
         @pl.when(direct)
         def _():
             for t in range(2):
-                send_half(0, t, nxt.at[0, 0, :, out_cut], next_sem.at[0], next_sem.at[1], sec + 1)
+                send_half(0, t, nxt.at[0, 0, :, out_cut], land_sem.at[0], sec + 1)
 
         @pl.when(jnp.logical_and(ours, jnp.logical_and(sec == 1, even)))
         def _():
             slot = core * (HALF // 2) + j // 2
             for t in range(2):
-                send_half(0, t, relay.at[slot], next_sem.at[0], relay_sem.at[slot], 3)
+                send_half(0, t, relay.at[slot], relay_sem, 3)
 
         @pl.when(jnp.logical_and(ours, jnp.logical_or(sec == 1, sec == 3)))
         def _():
             for t in range(2):
                 send_half(
-                    WIDE, t, ggate.at[0, 0, :, out_cut], gate_sem.at[0], gate_sem.at[1], sec - 1
+                    WIDE, t, ggate.at[0, 0, :, out_cut], land_sem.at[1], sec - 1
                 )
 
         @pl.when(jnp.logical_and(ours, sec == 2))
         def _():
             slot = core * HALF + j
             for t in range(2):
-                send_half(WIDE, t, relay.at[slot], gate_sem.at[0], relay_sem.at[slot], 0)
+                send_half(WIDE, t, relay.at[slot], relay_sem, 0)
 
         @pl.when(helping == 1)
         def _():
             ggate[0, 0, :, out_cut] = stage_o[j, tok : 2 * tok, WIDE : 2 * WIDE]
-            send_half(WIDE, 0, ggate.at[0, 0, :, out_cut], gate_sem.at[0], gate_sem.at[1], sec)
+            send_half(WIDE, 0, ggate.at[0, 0, :, out_cut], land_sem.at[1], sec)
 
         @pl.when(jnp.logical_and(helping == 1, sec < nsec - 2))
         def _():
             for t in range(2):
-                send_half(0, t, nxt.at[0, 0, :, out_cut], next_sem.at[0], next_sem.at[1], sec + 2)
-
+                send_half(0, t, nxt.at[0, 0, :, out_cut], land_sem.at[0], sec + 2)
+
+        partial[dp, slot_p, 6:8, :] = jnp.zeros((2, MIX), F32)
+        partial[dp, slot_p, 5:6, WIDE:MIX] = jnp.zeros((1, MIX - WIDE), F32)
         partial[dp, slot_p, 5:6, 0:WIDE] = jnp.sum(cot * normed, axis=0, keepdims=True)
         dyx = jnp.sum(dy * x, axis=0, keepdims=True)
         dscore = jnp.zeros((seq, seq), F32)
@@ -639,7 +640,7 @@
                 remote(
                     stage_c.at[j, pl.ds(0, tok), pl.ds(off, width)],
                     gconv.at[0, 0, :, pl.ds(start, width)],
-                    conv_sem.at[0], conv_sem.at[1], 0, sec, dp,
+                    land_sem.at[2], 0, sec, dp,
                 ).start()
 
             @pl.when(jnp.logical_and(ours, sec > 0))
@@ -648,7 +649,7 @@
                     remote(
                         stage_c.at[j, pl.ds(t * tok, tok), pl.ds(off, width)],
                         gconv.at[0, 0, :, pl.ds(start, width)],
-                        conv_sem.at[0], conv_sem.at[1], t, sec - 1, dp,
+                        land_sem.at[2], t, sec - 1, dp,
                     ).start()
 
         zpad[0:seq, WIDE + STATE : MIX] = dot3(ds_p, bmap, NN) * dsl[:, WIDE + STATE : MIX]
@@ -692,7 +693,7 @@
         def _():
             remote(
                 partial.at[dp, HALF + 1], partial.at[dp, HALF - 1],
-                hand_sem.at[0], hand_sem.at[1], core, sec + 1, dp,
+                hand_sem.at[0], core, sec + 1, dp,
             ).start()
 
         return 0
@@ -701,28 +702,25 @@
         for k in range(1, ndp):
             to = lax.rem(dp + k, ndp)
             remote(
-                partial.at[dp, slot], partial.at[dp, slot], ps_sem.at[to], pr_sem.at[dp],
-                core, sec, to,
+                partial.at[dp, slot], partial.at[dp, slot], sum_sem, core, sec, to
             ).start()
 
     lax.fori_loop(0, own_groups + helper, group, 0)
 
-    def pass_on(slot, g, out, landed, s):
-        part = relay.at[slot]
-        remote(part, part, via_sem.at[0], relay_sem.at[slot], core, s, dp).wait_recv()
-        remote(
-            part, out.at[0, 0, :, pl.ds(g * WIDE, WIDE)], via_sem.at[0], landed, core, s, dp
-        ).start()
+    def pass_on(slots, groups, out, sem, s):
+        landed(relay.at[pl.ds(0, slots)], relay_sem)
+        for slot, g in zip(range(slots), groups):
+            remote(
+                relay.at[slot], out.at[0, 0, :, pl.ds(g * WIDE, WIDE)], sem, core, s, dp
+            ).start()
 
     @pl.when(sec == 0)
     def _():
-        for g in range(GROUPS - 1):
-            pass_on(g, g, ggate, gate_sem.at[1], 1)
+        pass_on(GROUPS - 1, range(GROUPS - 1), ggate, land_sem.at[1], 1)
 
     @pl.when(sec == 3)
     def _():
-        for at in range(GROUPS // 2):
-            pass_on(at, 2 * at, nxt, next_sem.at[1], 2)
+        pass_on(GROUPS // 2, range(0, GROUPS, 2), nxt, land_sem.at[0], 2)
 
     @pl.when(sec == 0)
     def _():
@@ -752,7 +750,7 @@
         step_terms(1, small_out)
         small_out[2:3, 0:HEADS] = small[2:3, halves_of : halves_of + HEADS]
         remote(
-            small_out, small_in, hand_sem.at[2], hand_sem.at[3], core, sec + 1, dp
+            small_out, small_in, hand_sem.at[1], core, sec + 1, dp
         ).start()
 
     turned = drate[...].T
@@ -764,7 +762,7 @@
         for t in range(2):
             remote(
                 stage_s.at[t], step_parts.at[core],
-                dstep_sem.at[2], dstep_sem.at[core], t, sec - 1, dp,
+                dstep_sem.at[0], t, sec - 1, dp,
             ).start()
 
     @pl.when(helper == 1)
@@ -772,32 +770,26 @@
         stage_s[2] = turned[halves_of : halves_of + HEADS, 0:tok].astype(BF16)
         step_parts[2] = turned[halves_of : halves_of + HEADS, tok : 2 * tok].astype(BF16)
         remote(
-            stage_s.at[2], step_parts.at[2], dstep_sem.at[4], dstep_sem.at[3], other, sec, dp
+            stage_s.at[2], step_parts.at[2], dstep_sem.at[1], other, sec, dp
         ).start()
 
     @pl.when(donor == 1)
     def _():
-        landed = partial.at[dp, HALF - 1]
-        remote(landed, landed, hand_sem.at[0], hand_sem.at[1], core, sec - 1, dp).wait_recv()
+        landed(partial.at[dp, HALF - 1], hand_sem.at[0])
+        landed(small_in, hand_sem.at[1])
         spread(HALF - 1)
-        remote(small_in, small_in, hand_sem.at[2], hand_sem.at[3], core, sec - 1, dp).wait_recv()
         small[...] += small_in[...]
 
+    partial[dp, HALF] = jnp.zeros((8, MIX), F32)
     partial[dp, HALF, :, 0:128] = small[...]
     spread(HALF)
-    for k in range(1, ndp):
-        to = lax.rem(dp + k, ndp)
-        remote(
-            partial.at[dp, pl.ds(0, HALF + 1)], partial.at[to, pl.ds(0, HALF + 1)],
-            ps_sem.at[to], pr_sem.at[to], core, sec, to,
-        ).wait()
+    landed(partial.at[pl.ds(0, ndp - 1), pl.ds(0, HALF + 1)], sum_sem)
     total = partial[0, 0 : HALF + 1]
     for k in range(1, ndp):
         total = total + partial[k, 0 : HALF + 1]
     final[core] = total
-    halves = remote(final.at[core], final.at[core], fin_sem.at[0], fin_sem.at[1], other, sec, dp)
-    halves.start()
-    remote(final.at[core], final.at[other], fin_sem.at[0], fin_sem.at[1], other, sec, dp).wait()
+    remote(final.at[core], final.at[core], fin_sem, other, sec, dp).start()
+    landed(final.at[other], fin_sem)
     for g in range(GROUPS):
         c, j = g // HALF, g % HALF
         gng[0:1, g * WIDE : (g + 1) * WIDE] = final[c, j, 5:6, 0:WIDE]
@@ -813,87 +805,84 @@
 
     @pl.when(sec < nsec - 1)
     def _():
-        for c in range(2):
-            part = step_parts.at[c]
-            remote(part, part, dstep_sem.at[2], dstep_sem.at[c], core, sec + 1, dp).wait_recv()
+        landed(step_parts.at[pl.ds(0, 2)], dstep_sem.at[0])
 
         @pl.when(core == 0)
         def _():
-            part = step_parts.at[2]
-            remote(part, part, dstep_sem.at[4], dstep_sem.at[3], other, sec, dp).wait_recv()
+            landed(step_parts.at[2], dstep_sem.at[1])
 
         both = step_parts[0].astype(F32) + step_parts[1].astype(F32)
         gstep[0, 0] = (both + step_parts[2].astype(F32)).astype(BF16)
 
-    def sent(ref, sem):
-        remote(ref, ref, sem, sem, other, sec, dp).wait_send()
-
-    def landed(ref, sem):
-        remote(ref, ref, sem, sem, other, sec, dp).wait_recv()
-
-    def exchanged(j, _):
-        sent(uin.at[j, mine], xs_sem.at[j])
-        return 0
-
-    lax.fori_loop(0, HALF - other * gives, exchanged, 0)
     first = pl.ds(0, HALF - 1)
     half = pl.ds(0, WIDE)
+    sent(steps.at[0, 0])
+    sent(uin.at[first, pl.ds(0, tok)])
+    sent(partial.at[pl.ds(0, ndp - 1), pl.ds(0, HALF + 1)])
+    sent(final.at[0])
+
+    @pl.when(other * gives == 0)
+    def _():
+        sent(uin.at[0, pl.ds(0, tok)])
 
     @pl.when(sec == 0)
     def _():
-        sent(relay.at[pl.ds(0, GROUPS - 1)], via_sem.at[0])
+        sent(relay.at[pl.ds(0, GROUPS - 1)])
 
     @pl.when(sec == nsec - 1)
     def _():
-        sent(relay.at[pl.ds(0, GROUPS // 2)], via_sem.at[0])
+        sent(relay.at[pl.ds(0, GROUPS // 2)])
 
     @pl.when(sec > 0)
     def _():
-        sent(uin.at[HALF, pl.ds(0, tok)], ship_sem.at[0])
-        sent(steps.at[1, 0], ship_sem.at[1])
-        sent(stage_c.at[first], conv_sem.at[0])
-        sent(stage_o.at[first, :, half], gate_sem.at[0])
-        sent(stage_s.at[pl.ds(0, 2)], dstep_sem.at[2])
-        landed(nxt.at[0, 0], next_sem.at[1])
+        sent(uin.at[HALF, pl.ds(0, tok)])
+        sent(steps.at[1, 0])
+        sent(stage_c.at[first])
+        sent(stage_o.at[first, :, half])
+        sent(stage_s.at[pl.ds(0, 2)])
 
     @pl.when(jnp.logical_and(sec > 0, core == 0))
     def _():
         some = pl.ds(0, WIDE + 2 * STATE)
-        sent(w_ref.at[pl.ds(1, 1), :, some], ship_sem.at[2])
-        sent(b_ref.at[1, :, some], ship_sem.at[3])
-        sent(ng_ref.at[1, :, half], ship_sem.at[4])
-        sent(sb_ref.at[1], ship_sem.at[5])
-        sent(dl_ref.at[1], ship_sem.at[6])
-        sent(sk_ref.at[1], ship_sem.at[7])
-        sent(stage_c.at[HALF - 1], conv_sem.at[0])
-        sent(stage_o.at[HALF - 1, :, half], gate_sem.at[0])
+        for ref in (
+            w_ref.at[pl.ds(1, 1), :, some], b_ref.at[1, :, some], ng_ref.at[1, :, half],
+            per_head.at[1], stage_c.at[HALF - 1], stage_o.at[HALF - 1, :, half],
+        ):
+            sent(ref)
 
     @pl.when(sec < nsec - 1)
     def _():
-        sent(stage_o.at[first, :, half], next_sem.at[0])
+        sent(stage_o.at[first, :, half])
 
     @pl.when(jnp.logical_and(sec < nsec - 1, donor == 0))
     def _():
-        sent(stage_o.at[HALF - 1, :, half], next_sem.at[0])
+        sent(stage_o.at[HALF - 1, :, half])
 
     @pl.when(helper == 1)
     def _():
-        sent(stage_c.at[HALF, pl.ds(0, tok)], conv_sem.at[0])
-        sent(stage_o.at[HALF, pl.ds(0, tok), half], gate_sem.at[0])
-        sent(stage_s.at[2], dstep_sem.at[4])
-        sent(partial.at[dp, HALF + 1], hand_sem.at[0])
-        sent(small_out, hand_sem.at[2])
-        landed(ggate.at[0, 0, :, pl.ds(0, INNER - WIDE)], gate_sem.at[1])
-        landed(gconv.at[0, 0, :, pl.ds(0, (GROUPS - 1) * MIX)], conv_sem.at[1])
+        sent(stage_c.at[HALF, pl.ds(0, tok)])
+        sent(stage_o.at[HALF, pl.ds(0, tok), half])
+        sent(stage_s.at[2])
+        sent(partial.at[dp, HALF + 1])
+        sent(small_out)
 
     @pl.when(jnp.logical_and(helper == 1, sec < nsec - 2))
     def _():
-        sent(stage_o.at[HALF, :, half], next_sem.at[0])
+        sent(stage_o.at[HALF, :, half])
+
+    @pl.when(sec > 0)
+    def _():
+        landed(nxt.at[0, 0], land_sem.at[0])
+
+    @pl.when(helper == 1)
+    def _():
+        landed(ggate.at[0, 0, :, pl.ds(0, INNER - WIDE)], land_sem.at[1])
+        landed(gconv.at[0, 0, :, pl.ds(0, (GROUPS - 1) * MIX)], land_sem.at[2])
 
     @pl.when(jnp.logical_and(sec < nsec - 1, core == 0))
     def _():
-        landed(ggate.at[0, 0], gate_sem.at[1])
-        landed(gconv.at[0, 0], conv_sem.at[1])
+        landed(ggate.at[0, 0], land_sem.at[1])
+        landed(gconv.at[0, 0], land_sem.at[2])
 
 
 def finish_kernel(*refs):
@@ -918,9 +907,7 @@
     scratch = [
         pltpu.VMEM((2,) + conv_weight.shape[1:], F32),
         pltpu.VMEM((2,) + conv_bias.shape, F32),
-        pltpu.VMEM((2,) + step_bias.shape, F32),
-        pltpu.VMEM((2,) + decay_log.shape, F32),
-        pltpu.VMEM((2,) + skip_gain.shape, F32),
+        pltpu.VMEM((2, 3) + step_bias.shape, F32),
         pltpu.VMEM((2,) + norm_gain.shape, F32),
         pltpu.VMEM((HALF + 1, seq, MIX + 2 * WIDE), BF16),
         pltpu.VMEM((2, 2, HEADS, tok), BF16),
@@ -944,25 +931,10 @@
         pltpu.VMEM((8, 128), F32),
         pltpu.SemaphoreType.DMA((HALF,)),
         pltpu.SemaphoreType.DMA((HALF,)),
-        pltpu.SemaphoreType.DMA((HALF,)),
-        pltpu.SemaphoreType.DMA((3,)),
-        pltpu.SemaphoreType.DMA((2,)),
-        pltpu.SemaphoreType.DMA((2,)),
-        pltpu.SemaphoreType.DMA((2,)),
-        pltpu.SemaphoreType.DMA((5,)),
-        pltpu.SemaphoreType.DMA((ndp,)),
-        pltpu.SemaphoreType.DMA((ndp,)),
-        pltpu.SemaphoreType.DMA((2,)),
-        pltpu.SemaphoreType.DMA((1,)),
-        pltpu.SemaphoreType.DMA((GROUPS,)),
-        pltpu.SemaphoreType.DMA((6,)),
-        pltpu.SemaphoreType.REGULAR,
-        pltpu.SemaphoreType.REGULAR,
-        pltpu.SemaphoreType.REGULAR,
-        pltpu.SemaphoreType.DMA((8,)),
-        pltpu.SemaphoreType.DMA((8,)),
-        pltpu.SemaphoreType.DMA((4,)),
     ]
+    one = pltpu.SemaphoreType.DMA
+    scratch += [one, one((3,)), one((5,)), one, one((6,)), one, one((2,)), one, one((2,)), one]
+    scratch += [pltpu.SemaphoreType.REGULAR] * 3
     turned = jnp.swapaxes(step_input, 2, 3)
     shapes = [
         (gate_input.shape, BF16),

time: 44.6 us -> 44.2 us (level)
  no operation moved by 1% of the time
where the time goes in v5:
time: 44.2 us; the launch traced here: 44.1 us
  Pallas kernels  43.4 us (98%)
  between operations  0.65 us (1%)
    pallas_call x1, Pallas kernels, paired(): pl.pallas_call(pair_kernel, name='mixer_tick', in_specs=[hbm] * 10, out_s...  42.1 us
    pallas_call x1, Pallas kernels, paired(): pl.pallas_call(finish_kernel, name='mixer_finish', in_specs=[vmem] * 10,...  1.35 us

profile of v5, /device:TPU:0, one launch (start us, length us, event | category | flops | bytes accessed | tf_op | source)
XLA Modules:
  0.0 44.1 jit_solution(5366107704890799934)
XLA Ops:
  0.6 42.1 %mixer_tick.1 = (bf16[1,1,128,1024]{3,2,1,0:T(8,128)(2,1)S(1)}, bf16[1,1,128,5120]{3,2,1,0:T(8,128)(2,1)S(1)}, bf16[1,1,128,1024]{3,2,1,0:T(8,128)(2,1)S(1)}, bf...) custom-call(bf16[1,1,128,5120]{3,2,1,0:T(8,128)(2,1)} %conv_in.1, ...), custom_call_target="tpu_custom_call" | custom-call | tf_op jit(solution)/shard_map/mixer_tick/pallas_call | solution.py:958
  42.7 1.3 %mixer_finish.1 = (bf16[1,1,128,1024]{3,2,1,0:T(8,128)(2,1)}, bf16[1,1,128,5120]{3,2,1,0:T(8,128)(2,1)}, bf16[1,1,128,1024]{3,2,1,0:T(8,128)(2,1)}, bf16[1,1,16,...) custom-call(bf16[1,1,128,1024]{3,2,1,0:T(8,128)(2,1)S(1)} %get-tuple, ...), custom_call_target="tpu_custom_call" | custom-call | tf_op jit(solution)/shard_map/mixer_finish/pallas_call | solution.py:969

commit v6 on v5

--- a/solution.py
+++ b/solution.py
@@ -257,12 +257,12 @@
 
 def pair_kernel(
     conv_in, gate_in, step_in, cot_in, w_in, b_in, sb_in, dl_in, sk_in, ng_in,
-    nxt, gconv, ggate, gstep, gtap, gcb, gsb, gdl, gsk, gng,
+    rows_out, table_out, heads_out,
     w_ref, b_ref, per_head, ng_ref,
     uin, steps, token_rows, token_cols, upad, zpad, mix, dsl, ddt, drate, small,
     stage_c, stage_o, stage_s, step_parts, partial, final, relay, small_out, small_in,
     own_sem, xr_sem, sent_sem, land_sem, load_sem, step_sem, ship_sem, relay_sem, dstep_sem,
-    sum_sem, hand_sem, fin_sem, pair_sem, plane_sem, world_sem,
+    sum_sem, hand_sem, fin_sem, pair_sem, mate_sem, plane_sem, world_sem,
 ):
     core = lax.axis_index("ctx")
     sec = lax.axis_index("section")
@@ -292,17 +292,21 @@
     after = lax.rem(sec + 1, nsec)
     before = lax.rem(sec + nsec - 1, nsec)
     sb_ref, dl_ref, sk_ref = (per_head.at[:, at] for at in range(3))
+    nxt = rows_out.at[:, pl.ds(0, INNER)]
+    gconv = rows_out.at[:, pl.ds(INNER, 5 * INNER)]
+    ggate = rows_out.at[:, pl.ds(6 * INNER, INNER)]
+    gstep = rows_out.at[pl.ds(0, HEADS), pl.ds(7 * INNER, tok)]
     barrier = pltpu.get_barrier_semaphore()
 
     def greet(c, s, d):
         pl.semaphore_signal(barrier, inc=1, device_id=place(c, s, d), device_id_type=MESH)
 
-    for c in range(2):
-        for s in (1, 3):
-
-            @pl.when(jnp.logical_and(sec // 2 == s // 2, jnp.logical_or(sec != s, core != c)))
-            def _():
-                greet(c, s, dp)
+    upper = lax.rem(sec, 2) == 1
+
+    @pl.when(jnp.logical_not(upper))
+    def _():
+        for c in range(2):
+            greet(c, sec + 1, dp)
 
     def pieces(g):
         xc, bc, cc = group_columns(g)
@@ -316,14 +320,12 @@
 
     mine = pl.ds(pl.multiple_of(core * tok, tok), tok)
     theirs = pl.ds(pl.multiple_of(other * tok, tok), tok)
-    upper = lax.rem(sec, 2) == 1
-
-    def tell(sem, s):
-        pl.semaphore_signal(sem, inc=1, device_id=place(core, s, dp), device_id_type=MESH)
+    def tell(sem, s, c=core):
+        pl.semaphore_signal(sem, inc=1, device_id=place(c, s, dp), device_id_type=MESH)
 
     @pl.when(upper)
     def _():
-        pl.semaphore_wait(barrier, 3)
+        pl.semaphore_wait(barrier, 2)
 
     def landed(ref, sem):
         remote(ref, ref, sem, other, sec, dp).wait_recv()
@@ -353,12 +355,14 @@
 
     @pl.when(upper)
     def _():
-        tell(pair_sem, sec - 1)
         hand_over()
+        for c in range(2):
+            tell(pair_sem, sec - 1, c)
 
     @pl.when(sec == 1)
     def _():
-        greet(core, 2, dp)
+        for c in range(2):
+            greet(c, 2, dp)
 
     own_step = pltpu.make_async_copy(step_in.at[0, 0], steps.at[0, core], load_sem.at[0])
     own_step.start()
@@ -388,7 +392,12 @@
 
     @pl.when(jnp.logical_not(upper))
     def _():
-        pl.semaphore_wait(pair_sem, 1)
+        pl.semaphore_wait(pair_sem, 2)
+        tell(mate_sem, sec + 1)
+
+    @pl.when(upper)
+    def _():
+        pl.semaphore_wait(mate_sem, 1)
 
     remote(step_in.at[0, 0], steps.at[0, core], step_sem, other, sec, dp).start()
 
@@ -403,7 +412,7 @@
 
     @pl.when(sec == 2)
     def _():
-        pl.semaphore_wait(barrier, 1)
+        pl.semaphore_wait(barrier, 2)
         tell(plane_sem, 0)
         tell(plane_sem, 1)
         hand_over()
@@ -572,7 +581,7 @@
         @pl.when(direct)
         def _():
             for t in range(2):
-                send_half(0, t, nxt.at[0, 0, :, out_cut], land_sem.at[0], sec + 1)
+                send_half(0, t, nxt.at[:, out_cut], land_sem.at[0], sec + 1)
 
         @pl.when(jnp.logical_and(ours, jnp.logical_and(sec == 1, even)))
         def _():
@@ -584,7 +593,7 @@
         def _():
             for t in range(2):
                 send_half(
-                    WIDE, t, ggate.at[0, 0, :, out_cut], land_sem.at[1], sec - 1
+                    WIDE, t, ggate.at[:, out_cut], land_sem.at[1], sec - 1
                 )
 
         @pl.when(jnp.logical_and(ours, sec == 2))
@@ -595,13 +604,13 @@
 
         @pl.when(helping == 1)
         def _():
-            ggate[0, 0, :, out_cut] = stage_o[j, tok : 2 * tok, WIDE : 2 * WIDE]
-            send_half(WIDE, 0, ggate.at[0, 0, :, out_cut], land_sem.at[1], sec)
+            ggate[:, out_cut] = stage_o[j, tok : 2 * tok, WIDE : 2 * WIDE]
+            send_half(WIDE, 0, ggate.at[:, out_cut], land_sem.at[1], sec)
 
         @pl.when(jnp.logical_and(helping == 1, sec < nsec - 2))
         def _():
             for t in range(2):
-                send_half(0, t, nxt.at[0, 0, :, out_cut], land_sem.at[0], sec + 2)
+                send_half(0, t, nxt.at[:, out_cut], land_sem.at[0], sec + 2)
 
         partial[dp, slot_p, 6:8, :] = jnp.zeros((2, MIX), F32)
         partial[dp, slot_p, 5:6, WIDE:MIX] = jnp.zeros((1, MIX - WIDE), F32)
@@ -636,10 +645,10 @@
 
             @pl.when(helping == 1)
             def _():
-                gconv[0, 0, :, pl.ds(start, width)] = stage_c[j, tok : 2 * tok, off : off + width]
+                gconv[:, pl.ds(start, width)] = stage_c[j, tok : 2 * tok, off : off + width]
                 remote(
                     stage_c.at[j, pl.ds(0, tok), pl.ds(off, width)],
-                    gconv.at[0, 0, :, pl.ds(start, width)],
+                    gconv.at[:, pl.ds(start, width)],
                     land_sem.at[2], 0, sec, dp,
                 ).start()
 
@@ -648,7 +657,7 @@
                 for t in range(2):
                     remote(
                         stage_c.at[j, pl.ds(t * tok, tok), pl.ds(off, width)],
-                        gconv.at[0, 0, :, pl.ds(start, width)],
+                        gconv.at[:, pl.ds(start, width)],
                         land_sem.at[2], t, sec - 1, dp,
                     ).start()
 
@@ -711,7 +720,7 @@
         landed(relay.at[pl.ds(0, slots)], relay_sem)
         for slot, g in zip(range(slots), groups):
             remote(
-                relay.at[slot], out.at[0, 0, :, pl.ds(g * WIDE, WIDE)], sem, core, s, dp
+                relay.at[slot], out.at[:, pl.ds(g * WIDE, WIDE)], sem, core, s, dp
             ).start()
 
     @pl.when(sec == 0)
@@ -792,16 +801,16 @@
     landed(final.at[other], fin_sem)
     for g in range(GROUPS):
         c, j = g // HALF, g % HALF
-        gng[0:1, g * WIDE : (g + 1) * WIDE] = final[c, j, 5:6, 0:WIDE]
+        table_out[5:6, g * WIDE : (g + 1) * WIDE] = final[c, j, 5:6, 0:WIDE]
         for off, width, col in (
             (0, WIDE, g * WIDE),
             (WIDE, STATE, INNER + g * STATE),
             (WIDE + STATE, STATE, INNER + (GROUPS + g) * STATE),
         ):
-            gtap[0, :, col : col + width] = final[c, j, 0:CONV, off : off + width]
-            gcb[0:1, col : col + width] = final[c, j, CONV : CONV + 1, off : off + width]
-    for at, ref in enumerate((gsb, gdl, gsk)):
-        ref[...] = final[0, HALF, at : at + 1, 0:HEADS] + final[1, HALF, at : at + 1, 0:HEADS]
+            table_out[0:CONV, col : col + width] = final[c, j, 0:CONV, off : off + width]
+            table_out[CONV : CONV + 1, col : col + width] = final[c, j, CONV : CONV + 1, off : off + width]
+    for at in range(3):
+        heads_out[at] = final[0, HALF, at : at + 1, 0:HEADS] + final[1, HALF, at : at + 1, 0:HEADS]
 
     @pl.when(sec < nsec - 1)
     def _():
@@ -812,7 +821,7 @@
             landed(step_parts.at[2], dstep_sem.at[1])
 
         both = step_parts[0].astype(F32) + step_parts[1].astype(F32)
-        gstep[0, 0] = (both + step_parts[2].astype(F32)).astype(BF16)
+        gstep[...] = (both + step_parts[2].astype(F32)).astype(BF16)
 
     first = pl.ds(0, HALF - 1)
     half = pl.ds(0, WIDE)
@@ -872,23 +881,36 @@
 
     @pl.when(sec > 0)
     def _():
-        landed(nxt.at[0, 0], land_sem.at[0])
+        landed(nxt, land_sem.at[0])
 
     @pl.when(helper == 1)
     def _():
-        landed(ggate.at[0, 0, :, pl.ds(0, INNER - WIDE)], land_sem.at[1])
-        landed(gconv.at[0, 0, :, pl.ds(0, (GROUPS - 1) * MIX)], land_sem.at[2])
+        landed(ggate.at[:, pl.ds(0, INNER - WIDE)], land_sem.at[1])
+        landed(gconv.at[:, pl.ds(0, (GROUPS - 1) * MIX)], land_sem.at[2])
 
     @pl.when(jnp.logical_and(sec < nsec - 1, core == 0))
     def _():
-        landed(ggate.at[0, 0], land_sem.at[1])
-        landed(gconv.at[0, 0], land_sem.at[2])
-
-
-def finish_kernel(*refs):
-    count = len(refs) // 2
-    sem = refs[-1]
-    copies = [pltpu.make_async_copy(refs[i], refs[count + i], sem.at[i]) for i in range(count)]
+        landed(ggate, land_sem.at[1])
+        landed(gconv, land_sem.at[2])
+
+
+def finish_kernel(
+    rows_in, table_in, heads_in, nxt, gconv, ggate, gstep, gtap, gcb, gsb, gdl, gsk, gng, sem
+):
+    tok = rows_in.shape[0]
+    copies = [
+        (rows_in.at[:, pl.ds(INNER, 5 * INNER)], gconv.at[0, 0]),
+        (rows_in.at[:, pl.ds(0, INNER)], nxt.at[0, 0]),
+        (rows_in.at[:, pl.ds(6 * INNER, INNER)], ggate.at[0, 0]),
+        (table_in.at[pl.ds(0, CONV)], gtap.at[0]),
+        (table_in.at[pl.ds(CONV, 1)], gcb),
+        (table_in.at[pl.ds(CONV + 1, 1), pl.ds(0, INNER)], gng),
+        (rows_in.at[pl.ds(0, HEADS), pl.ds(7 * INNER, tok)], gstep.at[0, 0]),
+        (heads_in.at[0], gsb),
+        (heads_in.at[1], gdl),
+        (heads_in.at[2], gsk),
+    ]
+    copies = [pltpu.make_async_copy(a, b, sem.at[at]) for at, (a, b) in enumerate(copies)]
     for copy in copies:
         copy.start()
     for copy in copies:
@@ -934,7 +956,7 @@
     ]
     one = pltpu.SemaphoreType.DMA
     scratch += [one, one((3,)), one((5,)), one, one((6,)), one, one((2,)), one, one((2,)), one]
-    scratch += [pltpu.SemaphoreType.REGULAR] * 3
+    scratch += [pltpu.SemaphoreType.REGULAR] * 4
     turned = jnp.swapaxes(step_input, 2, 3)
     shapes = [
         (gate_input.shape, BF16),
@@ -959,8 +981,12 @@
         pair_kernel,
         name="mixer_tick",
         in_specs=[hbm] * 10,
-        out_specs=[vmem] * 10,
-        out_shape=[pltpu.VMEM(shape, kind) for shape, kind in shapes],
+        out_specs=[vmem] * 3,
+        out_shape=[
+            pltpu.VMEM((tok, 7 * INNER + tok), BF16),
+            pltpu.VMEM((8, conv_bias.shape[1]), F32),
+            pltpu.VMEM((3,) + step_bias.shape, F32),
+        ],
         scratch_shapes=scratch,
         compiler_params=pltpu.CompilerParams(
             collective_id=0, has_side_effects=True, vmem_limit_bytes=24 * 1024 * 1024
@@ -969,7 +995,7 @@
     done = pl.pallas_call(
         finish_kernel,
         name="mixer_finish",
-        in_specs=[vmem] * 10,
+        in_specs=[vmem] * 3,
         out_specs=[hbm] * 10,
         out_shape=[jax.ShapeDtypeStruct(shape, kind) for shape, kind in shapes],
         scratch_shapes=[pltpu.SemaphoreType.DMA((10,))],

time: 44.2 us -> 43.8 us (level)
  Pallas kernels: 43.4 us -> 42.7 us
    pallas_call x1, Pallas kernels: 42.1 us -> 41.4 us  [paired(): pl.pallas_call(pair_kernel, name='mixer_tick', in_specs=[hbm] * 10, out_s...]
where the time goes in v6:
time: 43.8 us; the launch traced here: 43.4 us
  Pallas kernels  42.7 us (97%)
  between operations  0.65 us (1%)
    pallas_call x1, Pallas kernels, paired(): pl.pallas_call(pair_kernel, name='mixer_tick', in_specs=[hbm] * 10, out_s...  41.4 us
    pallas_call x1, Pallas kernels, paired(): pl.pallas_call(finish_kernel, name='mixer_finish', in_specs=[vmem] * 3, o...  1.34 us

profile of v6, /device:TPU:0, one launch (start us, length us, event | category | flops | bytes accessed | tf_op | source)
XLA Modules:
  0.0 43.4 jit_solution(6897202646819101821)
XLA Ops:
  0.6 41.4 %mixer_tick.1 = (bf16[128,7296]{1,0:T(8,128)(2,1)S(1)}, f32[8,5120]{1,0:T(8,128)S(1)}, f32[3,1,16]{2,1,0:T(1,128)S(1)}) custom-call(bf16[1,1,128,5120]{3,2,1,0:T(8,128)(2,1)} %conv_in.1, bf16[1,1,128,1024]{3,2,1,0:T(8,128)(2,1)} %gate_in.1, bf16[1,1,16,128]{3,2,1,0:T(8,128)(2,1)} %bitcast.2, bf16[1,1,128,1024]{3,2,1,0:T(8,128)(2,1)} %cot_in.1, ...), custom_call_target="tpu_custom_call" | custom-call | tf_op jit(solution)/shard_map/mixer_tick/pallas_call | solution.py:980
  42.0 1.3 %mixer_finish.1 = (bf16[1,1,128,1024]{3,2,1,0:T(8,128)(2,1)}, bf16[1,1,128,5120]{3,2,1,0:T(8,128)(2,1)}, bf16[1,1,128,1024]{3,2,1,0:T(8,128)(2,1)}, bf16[1,1,16,...) custom-call(bf16[128,7296]{1,0:T(8,128)(2,1)S(1)} %get-tuple-element, ...), custom_call_target="tpu_custom_call" | custom-call | tf_op jit(solution)/shard_map/mixer_finish/pallas_call | solution.py:995

commit v7 on v6

--- a/solution.py
+++ b/solution.py
@@ -364,13 +364,16 @@
         for c in range(2):
             greet(c, 2, dp)
 
+    def later(j):
+        return (j + HALF - 1) // HALF
+
     own_step = pltpu.make_async_copy(step_in.at[0, 0], steps.at[0, core], load_sem.at[0])
     own_step.start()
 
     def fetch(j, _):
         for src, off, width in pieces(core * HALF + j):
             pltpu.make_async_copy(
-                src, uin.at[j, mine, pl.ds(off, width)], own_sem.at[j]
+                src, uin.at[j, mine, pl.ds(off, width)], own_sem.at[later(j)]
             ).start()
         return 0
 
@@ -404,7 +407,7 @@
     def exchange(j, _):
         for src, off, width in pieces(other * HALF + j):
             remote(
-                src, uin.at[j, mine, pl.ds(off, width)], xr_sem.at[j], other, sec, dp
+                src, uin.at[j, mine, pl.ds(off, width)], xr_sem.at[later(j)], other, sec, dp
             ).start()
         return 0
 
@@ -482,9 +485,18 @@
                 mix[pl.ds(start, count), here] = z * s
                 dsl[pl.ds(start, count), here] = s * (1.0 + z * (1.0 - s))
 
-        @pl.when(ours)
-        def _():
-            pltpu.make_async_copy(uin.at[j, mine], uin.at[j, mine], own_sem.at[j]).wait()
+        def arrived(at, rows, done):
+            @pl.when(j == 0)
+            def _():
+                done(uin.at[0, rows], at.at[0])
+
+            for count, case in ((HALF - 1, 0), (HALF - 2, 1)):
+
+                @pl.when(jnp.logical_and(j == 1, donor == case))
+                def _():
+                    done(uin.at[pl.ds(1, count), rows], at.at[1])
+
+        arrived(own_sem, mine, lambda ref, sem: pltpu.make_async_copy(ref, ref, sem).wait())
 
         @pl.when(helping == 1)
         def _():
@@ -511,9 +523,7 @@
         def _():
             token_terms(helping)
 
-        @pl.when(ours)
-        def _():
-            landed(uin.at[j, theirs], xr_sem.at[j])
+        arrived(xr_sem, theirs, landed)
 
         conv_rows(pl.multiple_of(other * tok, tok), tok, True)
         conv_rows(tok, 8, False)
@@ -581,7 +591,7 @@
         @pl.when(direct)
         def _():
             for t in range(2):
-                send_half(0, t, nxt.at[:, out_cut], land_sem.at[0], sec + 1)
+                send_half(0, t, nxt.at[:, out_cut], land_sem, sec + 1)
 
         @pl.when(jnp.logical_and(ours, jnp.logical_and(sec == 1, even)))
         def _():
@@ -593,7 +603,7 @@
         def _():
             for t in range(2):
                 send_half(
-                    WIDE, t, ggate.at[:, out_cut], land_sem.at[1], sec - 1
+                    WIDE, t, ggate.at[:, out_cut], land_sem, sec - 1
                 )
 
         @pl.when(jnp.logical_and(ours, sec == 2))
@@ -605,12 +615,12 @@
         @pl.when(helping == 1)
         def _():
             ggate[:, out_cut] = stage_o[j, tok : 2 * tok, WIDE : 2 * WIDE]
-            send_half(WIDE, 0, ggate.at[:, out_cut], land_sem.at[1], sec)
+            send_half(WIDE, 0, ggate.at[:, out_cut], land_sem, sec)
 
         @pl.when(jnp.logical_and(helping == 1, sec < nsec - 2))
         def _():
             for t in range(2):
-                send_half(0, t, nxt.at[:, out_cut], land_sem.at[0], sec + 2)
+                send_half(0, t, nxt.at[:, out_cut], land_sem, sec + 2)
 
         partial[dp, slot_p, 6:8, :] = jnp.zeros((2, MIX), F32)
         partial[dp, slot_p, 5:6, WIDE:MIX] = jnp.zeros((1, MIX - WIDE), F32)
@@ -649,7 +659,7 @@
                 remote(
                     stage_c.at[j, pl.ds(0, tok), pl.ds(off, width)],
                     gconv.at[:, pl.ds(start, width)],
-                    land_sem.at[2], 0, sec, dp,
+                    land_sem, 0, sec, dp,
                 ).start()
 
             @pl.when(jnp.logical_and(ours, sec > 0))
@@ -658,7 +668,7 @@
                     remote(
                         stage_c.at[j, pl.ds(t * tok, tok), pl.ds(off, width)],
                         gconv.at[:, pl.ds(start, width)],
-                        land_sem.at[2], t, sec - 1, dp,
+                        land_sem, t, sec - 1, dp,
                     ).start()
 
         zpad[0:seq, WIDE + STATE : MIX] = dot3(ds_p, bmap, NN) * dsl[:, WIDE + STATE : MIX]
@@ -725,11 +735,11 @@
 
     @pl.when(sec == 0)
     def _():
-        pass_on(GROUPS - 1, range(GROUPS - 1), ggate, land_sem.at[1], 1)
+        pass_on(GROUPS - 1, range(GROUPS - 1), ggate, land_sem, 1)
 
     @pl.when(sec == 3)
     def _():
-        pass_on(GROUPS // 2, range(0, GROUPS, 2), nxt, land_sem.at[0], 2)
+        pass_on(GROUPS // 2, range(0, GROUPS, 2), nxt, land_sem, 2)
 
     @pl.when(sec == 0)
     def _():
@@ -764,23 +774,23 @@
 
     turned = drate[...].T
     for t in range(2):
-        stage_s[t] = turned[0:HEADS, t * tok : (t + 1) * tok].astype(BF16)
+        for c in range(2):
+            stage_s[t, c] = turned[c * 8 : c * 8 + 8, t * tok : (t + 1) * tok].astype(BF16)
 
     @pl.when(sec > 0)
     def _():
         for t in range(2):
             remote(
-                stage_s.at[t], step_parts.at[core],
-                dstep_sem.at[0], t, sec - 1, dp,
+                stage_s.at[t, core], step_parts.at[0, core], dstep_sem, t, sec - 1, dp
             ).start()
 
     @pl.when(helper == 1)
     def _():
-        stage_s[2] = turned[halves_of : halves_of + HEADS, 0:tok].astype(BF16)
-        step_parts[2] = turned[halves_of : halves_of + HEADS, tok : 2 * tok].astype(BF16)
-        remote(
-            stage_s.at[2], step_parts.at[2], dstep_sem.at[1], other, sec, dp
-        ).start()
+        for c in range(2):
+            top = halves_of + c * 8
+            stage_s[2, c] = turned[top : top + 8, 0:tok].astype(BF16)
+            step_parts[1, c] = turned[top : top + 8, tok : 2 * tok].astype(BF16)
+        remote(stage_s.at[2], step_parts.at[1], dstep_sem, other, sec, dp).start()
 
     @pl.when(donor == 1)
     def _():
@@ -814,14 +824,17 @@
 
     @pl.when(sec < nsec - 1)
     def _():
-        landed(step_parts.at[pl.ds(0, 2)], dstep_sem.at[0])
-
         @pl.when(core == 0)
         def _():
-            landed(step_parts.at[2], dstep_sem.at[1])
-
-        both = step_parts[0].astype(F32) + step_parts[1].astype(F32)
-        gstep[...] = (both + step_parts[2].astype(F32)).astype(BF16)
+            landed(step_parts, dstep_sem)
+
+        @pl.when(core == 1)
+        def _():
+            landed(step_parts.at[0], dstep_sem)
+
+        for c in range(2):
+            both = step_parts[0, c].astype(F32) + step_parts[1, c].astype(F32)
+            gstep[c * 8 : c * 8 + 8, :] = both.astype(BF16)
 
     first = pl.ds(0, HALF - 1)
     half = pl.ds(0, WIDE)
@@ -848,7 +861,7 @@
         sent(steps.at[1, 0])
         sent(stage_c.at[first])
         sent(stage_o.at[first, :, half])
-        sent(stage_s.at[pl.ds(0, 2)])
+        sent(stage_s.at[0])
 
     @pl.when(jnp.logical_and(sec > 0, core == 0))
     def _():
@@ -879,19 +892,21 @@
     def _():
         sent(stage_o.at[HALF, :, half])
 
-    @pl.when(sec > 0)
-    def _():
-        landed(nxt, land_sem.at[0])
-
-    @pl.when(helper == 1)
-    def _():
-        landed(ggate.at[:, pl.ds(0, INNER - WIDE)], land_sem.at[1])
-        landed(gconv.at[:, pl.ds(0, (GROUPS - 1) * MIX)], land_sem.at[2])
-
-    @pl.when(jnp.logical_and(sec < nsec - 1, core == 0))
-    def _():
-        landed(ggate, land_sem.at[1])
-        landed(gconv, land_sem.at[2])
+    whole, less = 6 * INNER, 6 * (INNER - WIDE)
+
+    @pl.when(sec == nsec - 1)
+    def _():
+        landed(nxt, land_sem)
+
+    for c, columns in ((0, whole), (1, less)):
+
+        @pl.when(jnp.logical_and(sec == 0, core == c))
+        def _():
+            landed(rows_out.at[:, pl.ds(0, columns)], land_sem)
+
+        @pl.when(jnp.logical_and(sec * (nsec - 1 - sec) > 0, core == c))
+        def _():
+            landed(rows_out.at[:, pl.ds(0, INNER + columns)], land_sem)
 
 
 def finish_kernel(
@@ -944,18 +959,18 @@
         pltpu.VMEM((8, 128), F32),
         pltpu.VMEM((HALF + 1, seq, MIX), BF16),
         pltpu.VMEM((HALF + 1, seq, 2 * WIDE), BF16),
-        pltpu.VMEM((3, HEADS, tok), BF16),
-        pltpu.VMEM((3, HEADS, tok), BF16),
+        pltpu.VMEM((3, 2, HEADS // 2, tok), BF16),
+        pltpu.VMEM((2, 2, HEADS // 2, tok), BF16),
         pltpu.VMEM((ndp, HALF + 2, 8, MIX), F32),
         pltpu.VMEM((2, HALF + 1, 8, MIX), F32),
         pltpu.VMEM((GROUPS, tok, WIDE), BF16),
         pltpu.VMEM((8, 128), F32),
         pltpu.VMEM((8, 128), F32),
-        pltpu.SemaphoreType.DMA((HALF,)),
-        pltpu.SemaphoreType.DMA((HALF,)),
+        pltpu.SemaphoreType.DMA((2,)),
+        pltpu.SemaphoreType.DMA((2,)),
     ]
     one = pltpu.SemaphoreType.DMA
-    scratch += [one, one((3,)), one((5,)), one, one((6,)), one, one((2,)), one, one((2,)), one]
+    scratch += [one, one, one((5,)), one, one((6,)), one, one, one, one((2,)), one]
     scratch += [pltpu.SemaphoreType.REGULAR] * 4
     turned = jnp.swapaxes(step_input, 2, 3)
     shapes = [

time: 43.8 us -> 43.7 us (level)
  no operation moved by 1% of the time
where the time goes in v7:
time: 43.7 us; the launch traced here: 43.2 us
  Pallas kernels  42.6 us (97%)
  between operations  0.65 us (1%)
    pallas_call x1, Pallas kernels, paired(): pl.pallas_call(pair_kernel, name='mixer_tick', in_specs=[hbm] * 10, out_s...  41.2 us
    pallas_call x1, Pallas kernels, paired(): pl.pallas_call(finish_kernel, name='mixer_finish', in_specs=[vmem] * 3, o...  1.34 us

profile of v7, /device:TPU:0, one launch (start us, length us, event | category | flops | bytes accessed | tf_op | source)
XLA Modules:
  0.0 43.2 jit_solution(5311374281096829892)
XLA Ops:
  0.6 41.2 %mixer_tick.1 = (bf16[128,7296]{1,0:T(8,128)(2,1)S(1)}, f32[8,5120]{1,0:T(8,128)S(1)}, f32[3,1,16]{2,1,0:T(1,128)S(1)}) custom-call(bf16[1,1,128,5120]{3,2,1,0:T(8,128)(2,1)} %conv_in.1, bf16[1,1,128,1024]{3,2,1,0:T(8,128)(2,1)} %gate_in.1, bf16[1,1,16,128]{3,2,1,0:T(8,128)(2,1)} %bitcast.2, bf16[1,1,128,1024]{3,2,1,0:T(8,128)(2,1)} %cot_in.1, ...), custom_call_target="tpu_custom_call" | custom-call | tf_op jit(solution)/shard_map/mixer_tick/pallas_call | solution.py:995
  41.9 1.3 %mixer_finish.1 = (bf16[1,1,128,1024]{3,2,1,0:T(8,128)(2,1)}, bf16[1,1,128,5120]{3,2,1,0:T(8,128)(2,1)}, bf16[1,1,128,1024]{3,2,1,0:T(8,128)(2,1)}, bf16[1,1,16,...) custom-call(bf16[128,7296]{1,0:T(8,128)(2,1)S(1)} %get-tuple-element, ...), custom_call_target="tpu_custom_call" | custom-call | tf_op jit(solution)/shard_map/mixer_finish/pallas_call | solution.py:1010

commit v8 on v7

--- a/solution.py
+++ b/solution.py
@@ -393,6 +393,11 @@
     for ref in (token_rows, ddt, drate, small, small_out):
         ref[...] = jnp.zeros_like(ref)
 
+    @pl.when(sec == 2)
+    def _():
+        pl.semaphore_wait(barrier, 2)
+        hand_over()
+
     @pl.when(jnp.logical_not(upper))
     def _():
         pl.semaphore_wait(pair_sem, 2)
@@ -415,10 +420,8 @@
 
     @pl.when(sec == 2)
     def _():
-        pl.semaphore_wait(barrier, 2)
         tell(plane_sem, 0)
         tell(plane_sem, 1)
-        hand_over()
 
     @pl.when(jnp.logical_and(sec > 0, core == 0))
     def _():

time: 43.7 us -> 43.7 us (level)
  no operation moved by 1% of the time
where the time goes in v8:
time: 43.7 us; the launch traced here: 43.2 us
  Pallas kernels  42.6 us (97%)
  between operations  0.65 us (1%)
    pallas_call x1, Pallas kernels, paired(): pl.pallas_call(pair_kernel, name='mixer_tick', in_specs=[hbm] * 10, out_s...  41.2 us
    pallas_call x1, Pallas kernels, paired(): pl.pallas_call(finish_kernel, name='mixer_finish', in_specs=[vmem] * 3, o...  1.34 us

profile of v8, /device:TPU:0, one launch (start us, length us, event | category | flops | bytes accessed | tf_op | source)
XLA Modules:
  0.0 43.2 jit_solution(14143963061342191832)
XLA Ops:
  0.6 41.2 %mixer_tick.1 = (bf16[128,7296]{1,0:T(8,128)(2,1)S(1)}, f32[8,5120]{1,0:T(8,128)S(1)}, f32[3,1,16]{2,1,0:T(1,128)S(1)}) custom-call(bf16[1,1,128,5120]{3,2,1,0:T(8,128)(2,1)} %conv_in.1, bf16[1,1,128,1024]{3,2,1,0:T(8,128)(2,1)} %gate_in.1, bf16[1,1,16,128]{3,2,1,0:T(8,128)(2,1)} %bitcast.2, bf16[1,1,128,1024]{3,2,1,0:T(8,128)(2,1)} %cot_in.1, ...), custom_call_target="tpu_custom_call" | custom-call | tf_op jit(solution)/shard_map/mixer_tick/pallas_call | solution.py:998
  41.9 1.3 %mixer_finish.1 = (bf16[1,1,128,1024]{3,2,1,0:T(8,128)(2,1)}, bf16[1,1,128,5120]{3,2,1,0:T(8,128)(2,1)}, bf16[1,1,128,1024]{3,2,1,0:T(8,128)(2,1)}, bf16[1,1,16,...) custom-call(bf16[128,7296]{1,0:T(8,128)(2,1)S(1)} %get-tuple-element, ...), custom_call_target="tpu_custom_call" | custom-call | tf_op jit(solution)/shard_map/mixer_finish/pallas_call | solution.py:1013

commit v9 on v8

--- a/solution.py
+++ b/solution.py
@@ -599,8 +599,15 @@
         @pl.when(jnp.logical_and(ours, jnp.logical_and(sec == 1, even)))
         def _():
             slot = core * (HALF // 2) + j // 2
-            for t in range(2):
-                send_half(0, t, relay.at[slot], relay_sem, 3)
+            send_half(0, 0, relay.at[slot], relay_sem, 3)
+
+            @pl.when(core + j > 0)
+            def _():
+                send_half(0, 1, relay.at[slot], relay_sem, 3)
+
+            @pl.when(core + j == 0)
+            def _():
+                send_half(0, 1, nxt.at[:, out_cut], land_sem, 2)
 
         @pl.when(jnp.logical_and(ours, jnp.logical_or(sec == 1, sec == 3)))
         def _():
@@ -730,19 +737,21 @@
     lax.fori_loop(0, own_groups + helper, group, 0)
 
     def pass_on(slots, groups, out, sem, s):
-        landed(relay.at[pl.ds(0, slots)], relay_sem)
-        for slot, g in zip(range(slots), groups):
+        landed(relay.at[pl.ds(slots[0], len(slots))], relay_sem)
+        for slot, g in zip(slots, groups):
             remote(
                 relay.at[slot], out.at[:, pl.ds(g * WIDE, WIDE)], sem, core, s, dp
             ).start()
 
     @pl.when(sec == 0)
     def _():
-        pass_on(GROUPS - 1, range(GROUPS - 1), ggate, land_sem, 1)
-
-    @pl.when(sec == 3)
-    def _():
-        pass_on(GROUPS // 2, range(0, GROUPS, 2), nxt, land_sem, 2)
+        pass_on(range(GROUPS - 1), range(GROUPS - 1), ggate, land_sem, 1)
+
+    for c in range(2):
+
+        @pl.when(jnp.logical_and(sec == 3, core == c))
+        def _():
+            pass_on(range(c, GROUPS // 2), range(2 * c, GROUPS, 2), nxt, land_sem, 2)
 
     @pl.when(sec == 0)
     def _():
@@ -854,9 +863,11 @@
     def _():
         sent(relay.at[pl.ds(0, GROUPS - 1)])
 
-    @pl.when(sec == nsec - 1)
-    def _():
-        sent(relay.at[pl.ds(0, GROUPS // 2)])
+    for c in range(2):
+
+        @pl.when(jnp.logical_and(sec == nsec - 1, core == c))
+        def _():
+            sent(relay.at[pl.ds(c, GROUPS // 2 - c)])
 
     @pl.when(sec > 0)
     def _():

time: 43.7 us -> 43.8 us (level)
  no operation moved by 1% of the time
where the time goes in v9:
time: 43.8 us; the launch traced here: 43.6 us
  Pallas kernels  42.9 us (98%)
  between operations  0.65 us (1%)
    pallas_call x1, Pallas kernels, paired(): pl.pallas_call(pair_kernel, name='mixer_tick', in_specs=[hbm] * 10, out_s...  41.6 us
    pallas_call x1, Pallas kernels, paired(): pl.pallas_call(finish_kernel, name='mixer_finish', in_specs=[vmem] * 3, o...  1.34 us

profile of v9, /device:TPU:0, one launch (start us, length us, event | category | flops | bytes accessed | tf_op | source)
XLA Modules:
  0.0 43.6 jit_solution(6354173433810475974)
XLA Ops:
  0.6 41.6 %mixer_tick.1 = (bf16[128,7296]{1,0:T(8,128)(2,1)S(1)}, f32[8,5120]{1,0:T(8,128)S(1)}, f32[3,1,16]{2,1,0:T(1,128)S(1)}) custom-call(bf16[1,1,128,5120]{3,2,1,0:T(8,128)(2,1)} %conv_in.1, bf16[1,1,128,1024]{3,2,1,0:T(8,128)(2,1)} %gate_in.1, bf16[1,1,16,128]{3,2,1,0:T(8,128)(2,1)} %bitcast.2, bf16[1,1,128,1024]{3,2,1,0:T(8,128)(2,1)} %cot_in.1, ...), custom_call_target="tpu_custom_call" | custom-call | tf_op jit(solution)/shard_map/mixer_tick/pallas_call | solution.py:1009
  42.3 1.3 %mixer_finish.1 = (bf16[1,1,128,1024]{3,2,1,0:T(8,128)(2,1)}, bf16[1,1,128,5120]{3,2,1,0:T(8,128)(2,1)}, bf16[1,1,128,1024]{3,2,1,0:T(8,128)(2,1)}, bf16[1,1,16,...) custom-call(bf16[128,7296]{1,0:T(8,128)(2,1)S(1)} %get-tuple-element, ...), custom_call_target="tpu_custom_call" | custom-call | tf_op jit(solution)/shard_map/mixer_finish/pallas_call | solution.py:1024
